TPU v7x, 32 devices: a whole 2x2x4 slice. The times are simulated.
32 devices in a mesh: batch: 8 (over z, x), row: 2 (over y), col: 2 (over core).
Axes of the slice: x: 2, y: 2, z: 4, core: 2. Of those that a mesh axis runs over, the one named last changes fastest.
Arguments:
- patches: float32 [8, 2, 2, 16, 256], P('batch', 'row', 'col'), may hold values from -6 to 6
- cond: float32 [8, 4, 384], P('batch'), may hold values from -6 to 6
- image_lengths: int32 [8, 1, 4], P('batch'), may hold values from 0 to 1024, as said below
- cotangent: float32 [8, 2, 2, 32, 256], P('batch', 'row', 'col'), may hold values from -6 to 6
- w_patch: float32 [16, 384], replicated, may hold values from -1.5 to 1.5
- b_patch: float32 [384], replicated, may hold values from -1.75 to 1.75
- w_mod: float32 [384, 2304], replicated, may hold values from -0.3125 to 0.3125
- b_mod: float32 [2304], replicated, may hold values from -1.75 to 1.75
- w_qkv: float32 [384, 1152], replicated, may hold values from -0.3125 to 0.3125
- b_query: float32 [384], replicated, may hold values from -1.75 to 1.75
- b_value: float32 [384], replicated, may hold values from -1.75 to 1.75
- w_proj: float32 [384, 384], replicated, may hold values from -1.75 to 1.75
- b_proj: float32 [384], replicated, may hold values from -1.75 to 1.75
- w_fc1: float32 [384, 1536], replicated, may hold values from -0.3125 to 0.3125
- b_fc1: float32 [1536], replicated, may hold values from -1.75 to 1.75
- w_fc2: float32 [1536, 384], replicated, may hold values from -0.15625 to 0.15625
- b_fc2: float32 [384], replicated, may hold values from -1.75 to 1.75
- w_fmod: float32 [384, 768], replicated, may hold values from -0.3125 to 0.3125
- b_fmod: float32 [768], replicated, may hold values from -1.75 to 1.75
- w_out: float32 [384, 32], replicated, may hold values from -0.3125 to 0.3125
- b_out: float32 [32], replicated, may hold values from -1.75 to 1.75
Outputs:
- output: float32 [8, 2, 2, 32, 256], P('batch', 'row', 'col')
- grad_patches: float32 [8, 2, 2, 16, 256], P('batch', 'row', 'col')
- grad_cond: float32 [8, 4, 384], P('batch')
- grad_w_patch: float32 [16, 384], replicated
- grad_b_patch: float32 [384], replicated
- grad_w_mod: float32 [384, 2304], replicated
- grad_b_mod: float32 [2304], replicated
- grad_w_qkv: float32 [384, 1152], replicated
- grad_b_query: float32 [384], replicated
- grad_b_value: float32 [384], replicated
- grad_w_proj: float32 [384, 384], replicated
- grad_b_proj: float32 [384], replicated
- grad_w_fc1: float32 [384, 1536], replicated
- grad_b_fc1: float32 [1536], replicated
- grad_w_fc2: float32 [1536, 384], replicated
- grad_b_fc2: float32 [384], replicated
- grad_w_fmod: float32 [384, 768], replicated
- grad_b_fmod: float32 [768], replicated
- grad_w_out: float32 [384, 32], replicated
- grad_b_out: float32 [32], replicated
Inputs may be any that keep to these rules, and one draw needn't show every extreme that they name: `image_lengths`: each pack holds either one image of 1024 tokens followed by empty slots of length 0, or 4 images of 256 tokens; the lengths of a pack add up to 1024.
All inputs are finite; a program needn't handle non-finite values.
Results may differ from a plain program's by a relative error of at most 0.012.
The roundings to bfloat16 on the way count: a program that leaves them out, or rounds other values in their place, can miss the bound.
Values may be sent and summed in bfloat16 or wider, within the bound.
No kernel may reach another device: no remote copies, remote signals or barrier semaphores. Data moves between devices by JAX's collectives and lax.ppermute only.
A program may use at most 128 MiB of HBM per device.

v0:
```python
import math

import jax
import jax.numpy as jnp
from jax import lax
from jax.sharding import PartitionSpec as P

HEADS = 6
HEAD_DIM = 64
BIG_SIDE = 16
SMALL_SIDE = 8
BIG_LEN = 1024


exact_mode = lax.Precision.HIGHEST
eps_norm = 1e-06


def tile_layout(lengths, tile_row, tile_col, count_here, tile_count):
    tile_len = lengths // tile_count
    ends_at = jnp.cumsum(tile_len)
    starts_at = ends_at - tile_len
    place_index = jnp.arange(count_here, dtype=jnp.int32)
    segment = jnp.sum((place_index[:, None] >= ends_at[None, :]).astype(jnp.int32), axis=1)
    slot_index = jnp.arange(lengths.shape[0], dtype=jnp.int32)
    member = segment[:, None] == slot_index[None, :]
    slot_side = jnp.where(lengths == BIG_LEN, BIG_SIDE, SMALL_SIDE).astype(jnp.int32)
    token_side = jnp.sum(jnp.where(member, slot_side[None, :], 0), axis=1)
    token_start = jnp.sum(jnp.where(member, starts_at[None, :], 0), axis=1)
    offset_in = place_index - token_start
    grid_row = tile_row * token_side + offset_in // token_side
    grid_col = tile_col * token_side + offset_in % token_side
    return (segment, member.astype(jnp.float32), grid_row, grid_col)


def sincos_embed(grid_row, grid_col, model_width):
    quarter = model_width // 4
    rates = 1.0 / jnp.power(10000.0, jnp.arange(quarter, dtype=jnp.float32) / quarter)
    row_angle = grid_row.astype(jnp.float32)[:, None] * rates[None, :]
    col_angle = grid_col.astype(jnp.float32)[:, None] * rates[None, :]
    return jnp.concatenate(
        [jnp.sin(row_angle), jnp.cos(row_angle), jnp.sin(col_angle), jnp.cos(col_angle)], axis=1
    )


def gelu_tanh(values):
    return (
        0.5
        * values
        * (1.0 + jnp.tanh(0.7978845608028654 * (values + 0.044715 * values * values * values)))
    )


def norm_stats(values):
    center = values - jnp.mean(values, axis=1, keepdims=True)
    inv_std = lax.rsqrt(jnp.mean(center * center, axis=1, keepdims=True) + eps_norm)
    return (center * inv_std, inv_std)


def norm_back(grad_in, normed, inv_std):
    return inv_std * (
        grad_in
        - jnp.mean(grad_in, axis=1, keepdims=True)
        - normed * jnp.mean(grad_in * normed, axis=1, keepdims=True)
    )


def contract_rows(left_op, right_op):
    return lax.dot_general(
        left_op, right_op, (((0,), (0,)), ((), ())), preferred_element_type=jnp.float32
    )


def contract_last(left_op, right_op):
    return lax.dot_general(
        left_op, right_op, (((1,), (1,)), ((), ())), preferred_element_type=jnp.float32
    )


def column_block(array, index, model_width):
    return array[:, index * model_width : (index + 1) * model_width]


def heads_of(values):
    return values.reshape(values.shape[0], HEADS, HEAD_DIM)


def body(
    patches,
    cond,
    image_lengths,
    cotangent,
    w_patch,
    b_patch,
    w_mod,
    b_mod,
    w_qkv,
    b_query,
    b_value,
    w_proj,
    b_proj,
    w_fc1,
    b_fc1,
    w_fc2,
    b_fc2,
    w_fmod,
    b_fmod,
    w_out,
    b_out,
):
    model_width = w_patch.shape[1]
    pack_count = image_lengths.shape[1]
    slot_count = image_lengths.shape[2]
    token_count = patches.shape[4]
    tile_tokens = token_count // pack_count
    tile_count = lax.axis_size("row") * lax.axis_size("col")
    tile_row = lax.axis_index("row")
    tile_col = lax.axis_index("col")
    score_scale = 1.0 / math.sqrt(HEAD_DIM)

    def layout_pack(pack_lengths):
        return tile_layout(pack_lengths, tile_row, tile_col, tile_tokens, tile_count)

    segment, member, grid_row, grid_col = jax.vmap(layout_pack)(image_lengths[0])
    segment_all = jnp.tile(segment, (1, tile_count))
    position = sincos_embed(
        grid_row.reshape(token_count), grid_col.reshape(token_count), model_width
    )
    cond_slots = cond[0].reshape(pack_count, slot_count, model_width)
    act_cond = jax.nn.silu(cond_slots)
    mods_img = jnp.einsum("psd,de->pse", act_cond, w_mod, precision=exact_mode) + b_mod
    fmods_img = jnp.einsum("psd,de->pse", act_cond, w_fmod, precision=exact_mode) + b_fmod
    mods_tok = jnp.einsum("pts,pse->pte", member, mods_img, precision=exact_mode).reshape(
        token_count, 6 * model_width
    )
    fmods_tok = jnp.einsum("pts,pse->pte", member, fmods_img, precision=exact_mode).reshape(
        token_count, 2 * model_width
    )

    def score_block(q_heads, k_heads, seg_query, seg_key):
        scores = (
            jnp.einsum("qhd,khd->hqk", q_heads, k_heads, preferred_element_type=jnp.float32)
            * score_scale
        )
        return jnp.where((seg_query[:, None] == seg_key[None, :])[None], scores, -1e30)

    def attend_forward(packed):
        q_pack, k_pack, v_pack, seg_query, seg_key = packed
        scores = score_block(heads_of(q_pack), heads_of(k_pack), seg_query, seg_key)
        row_top = jnp.max(scores, axis=2, keepdims=True)
        exp_scores = jnp.exp(scores - row_top)
        row_total = jnp.sum(exp_scores, axis=2, keepdims=True)
        attn_low = (exp_scores / row_total).astype(jnp.bfloat16)
        mixed = jnp.einsum(
            "hqk,khd->qhd", attn_low, heads_of(v_pack), preferred_element_type=jnp.float32
        )
        return (
            mixed.reshape(q_pack.shape[0], model_width),
            (row_top + jnp.log(row_total))[:, :, 0],
        )

    def query_core(q_pack, k_pack, v_pack, do_pack, log_pack, seg_query, seg_key):
        attn_probs = jnp.exp(
            score_block(heads_of(q_pack), heads_of(k_pack), seg_query, seg_key)
            - log_pack[:, :, None]
        )
        grad_probs = jnp.einsum(
            "qhd,khd->hqk", heads_of(do_pack), heads_of(v_pack), preferred_element_type=jnp.float32
        )
        row_delta = jnp.sum(attn_probs * grad_probs, axis=2)
        grad_scores = (attn_probs * (grad_probs - row_delta[:, :, None])).astype(jnp.bfloat16)
        grad_query = (
            jnp.einsum(
                "hqk,khd->qhd", grad_scores, heads_of(k_pack), preferred_element_type=jnp.float32
            )
            * score_scale
        )
        return (
            grad_query.reshape(q_pack.shape[0], model_width),
            row_delta,
            grad_scores,
            attn_probs,
        )

    def full_side(packed):
        q_pack, k_pack, v_pack, do_pack, log_pack, seg_query, seg_key = packed
        grad_query, row_delta, grad_scores, attn_probs = query_core(
            q_pack, k_pack, v_pack, do_pack, log_pack, seg_query, seg_key
        )
        grad_keys = (
            jnp.einsum(
                "hqk,qhd->khd", grad_scores, heads_of(q_pack), preferred_element_type=jnp.float32
            )
            * score_scale
        )
        grad_values = jnp.einsum(
            "hqk,qhd->khd",
            attn_probs.astype(jnp.bfloat16),
            heads_of(do_pack),
            preferred_element_type=jnp.float32,
        )
        key_total = k_pack.shape[0]
        return (
            grad_query,
            grad_keys.reshape(key_total, model_width),
            grad_values.reshape(key_total, model_width),
        )

    patch_cols = patches[0, 0, 0]
    hidden_in = (
        lax.dot_general(
            patch_cols,
            w_patch,
            (((0,), (0,)), ((), ())),
            precision=exact_mode,
            preferred_element_type=jnp.float32,
        )
        + b_patch
        + position
    )
    normed_one, inv_one = norm_stats(hidden_in)
    scale_one = column_block(mods_tok, 1, model_width)
    entry_one = (normed_one * (1.0 + scale_one) + column_block(mods_tok, 0, model_width)).astype(
        jnp.bfloat16
    )
    w_qkv_low = w_qkv.astype(jnp.bfloat16)
    projected = jnp.dot(entry_one, w_qkv_low, preferred_element_type=jnp.float32)
    query_low = (column_block(projected, 0, model_width) + b_query).astype(jnp.bfloat16)
    keys_low = column_block(projected, 1, model_width).astype(jnp.bfloat16)
    values_low = (column_block(projected, 2, model_width) + b_value).astype(jnp.bfloat16)
    query_tiles = query_low.reshape(pack_count, tile_tokens, model_width)
    key_tiles = keys_low.reshape(pack_count, tile_tokens, model_width)
    value_tiles = values_low.reshape(pack_count, tile_tokens, model_width)
    key_all, value_all = (
        lax.all_gather(key_tiles, ("row", "col"), axis=1, tiled=True),
        lax.all_gather(value_tiles, ("row", "col"), axis=1, tiled=True),
    )
    attended, log_total = lax.map(
        attend_forward, (query_tiles, key_all, value_all, segment, segment_all)
    )
    attended_low = attended.reshape(token_count, model_width).astype(jnp.bfloat16)
    w_proj_low = w_proj.astype(jnp.bfloat16)
    attn_out = jnp.dot(attended_low, w_proj_low, preferred_element_type=jnp.float32) + b_proj
    gate_attn = column_block(mods_tok, 2, model_width)
    hidden_mid = hidden_in + gate_attn * attn_out
    normed_two, inv_two = norm_stats(hidden_mid)
    scale_two = column_block(mods_tok, 4, model_width)
    entry_two = (normed_two * (1.0 + scale_two) + column_block(mods_tok, 3, model_width)).astype(
        jnp.bfloat16
    )
    w_fc1_low = w_fc1.astype(jnp.bfloat16)
    w_fc2_low = w_fc2.astype(jnp.bfloat16)
    inner_pre = jnp.dot(entry_two, w_fc1_low, preferred_element_type=jnp.float32) + b_fc1
    activ_low = gelu_tanh(inner_pre).astype(jnp.bfloat16)
    mlp_out = jnp.dot(activ_low, w_fc2_low, preferred_element_type=jnp.float32) + b_fc2
    gate_mlp = column_block(mods_tok, 5, model_width)
    hidden_out = hidden_mid + gate_mlp * mlp_out
    normed_three, inv_three = norm_stats(hidden_out)
    scale_three = column_block(fmods_tok, 1, model_width)
    entry_three = (
        normed_three * (1.0 + scale_three) + column_block(fmods_tok, 0, model_width)
    ).astype(jnp.bfloat16)
    w_out_low = w_out.astype(jnp.bfloat16)
    result_cols = (
        lax.dot_general(
            w_out_low, entry_three, (((0,), (1,)), ((), ())), preferred_element_type=jnp.float32
        )
        + b_out[:, None]
    )
    grad_out_low = cotangent[0, 0, 0].astype(jnp.bfloat16)
    grad_w_out = lax.dot_general(
        entry_three, grad_out_low, (((0,), (1,)), ((), ())), preferred_element_type=jnp.float32
    )
    grad_b_out = jnp.sum(grad_out_low.astype(jnp.float32), axis=1)
    grad_entry_three = lax.dot_general(
        grad_out_low, w_out_low, (((0,), (1,)), ((), ())), preferred_element_type=jnp.float32
    )
    grad_fmods_tok = jnp.concatenate([grad_entry_three, grad_entry_three * normed_three], axis=1)
    grad_hidden_out = norm_back(grad_entry_three * (1.0 + scale_three), normed_three, inv_three)
    grad_mlp_low = (gate_mlp * grad_hidden_out).astype(jnp.bfloat16)
    grad_gate_mlp = grad_hidden_out * mlp_out
    grad_w_fc2 = contract_rows(activ_low, grad_mlp_low)
    grad_b_fc2 = jnp.sum(grad_mlp_low.astype(jnp.float32), axis=0)
    grad_activ = contract_last(grad_mlp_low, w_fc2_low)
    grad_inner_low = jax.vjp(gelu_tanh, inner_pre)[1](grad_activ)[0].astype(jnp.bfloat16)
    grad_w_fc1 = contract_rows(entry_two, grad_inner_low)
    grad_b_fc1 = jnp.sum(grad_inner_low.astype(jnp.float32), axis=0)
    grad_entry_two = contract_last(grad_inner_low, w_fc1_low)
    grad_hidden_mid = grad_hidden_out + norm_back(
        grad_entry_two * (1.0 + scale_two), normed_two, inv_two
    )
    grad_attn_low = (gate_attn * grad_hidden_mid).astype(jnp.bfloat16)
    grad_gate_attn = grad_hidden_mid * attn_out
    grad_w_proj = contract_rows(attended_low, grad_attn_low)
    grad_b_proj = jnp.sum(grad_attn_low.astype(jnp.float32), axis=0)
    grad_attended_low = contract_last(grad_attn_low, w_proj_low).astype(jnp.bfloat16)
    grad_att_tiles = grad_attended_low.reshape(pack_count, tile_tokens, model_width)
    grad_query, grad_keys_all, grad_values_all = lax.map(
        full_side,
        (query_tiles, key_all, value_all, grad_att_tiles, log_total, segment, segment_all),
    )
    grad_keys, grad_values = (
        lax.psum_scatter(grad_keys_all, ("row", "col"), scatter_dimension=1, tiled=True),
        lax.psum_scatter(grad_values_all, ("row", "col"), scatter_dimension=1, tiled=True),
    )
    grad_query_low = grad_query.reshape(token_count, model_width).astype(jnp.bfloat16)
    grad_keys_low = grad_keys.reshape(token_count, model_width).astype(jnp.bfloat16)
    grad_values_low = grad_values.reshape(token_count, model_width).astype(jnp.bfloat16)
    grad_qkv = jnp.concatenate([grad_query_low, grad_keys_low, grad_values_low], axis=1)
    grad_w_qkv = contract_rows(entry_one, grad_qkv)
    grad_b_query = jnp.sum(grad_query_low.astype(jnp.float32), axis=0)
    grad_b_value = jnp.sum(grad_values_low.astype(jnp.float32), axis=0)
    grad_entry_one = contract_last(grad_qkv, w_qkv_low)
    grad_hidden_in = grad_hidden_mid + norm_back(
        grad_entry_one * (1.0 + scale_one), normed_one, inv_one
    )
    grad_w_patch = lax.dot_general(
        patch_cols,
        grad_hidden_in,
        (((1,), (0,)), ((), ())),
        precision=exact_mode,
        preferred_element_type=jnp.float32,
    )
    grad_b_patch = jnp.sum(grad_hidden_in, axis=0)
    grad_patch_cols = lax.dot_general(
        w_patch,
        grad_hidden_in,
        (((1,), (1,)), ((), ())),
        precision=exact_mode,
        preferred_element_type=jnp.float32,
    )
    grad_mods_tok = jnp.concatenate(
        [
            grad_entry_one,
            grad_entry_one * normed_one,
            grad_gate_attn,
            grad_entry_two,
            grad_entry_two * normed_two,
            grad_gate_mlp,
        ],
        axis=1,
    )
    grad_mods_img = jnp.einsum(
        "pts,pte->pse",
        member,
        grad_mods_tok.reshape(pack_count, tile_tokens, 6 * model_width),
        precision=exact_mode,
    )
    grad_fmods_img = jnp.einsum(
        "pts,pte->pse",
        member,
        grad_fmods_tok.reshape(pack_count, tile_tokens, 2 * model_width),
        precision=exact_mode,
    )
    slot_total = pack_count * slot_count
    grad_w_mod = jnp.einsum("psd,pse->de", act_cond, grad_mods_img, precision=exact_mode)
    grad_b_mod = jnp.sum(grad_mods_img, axis=(0, 1))
    grad_w_fmod = jnp.einsum("psd,pse->de", act_cond, grad_fmods_img, precision=exact_mode)
    grad_b_fmod = jnp.sum(grad_fmods_img, axis=(0, 1))
    grad_act = jnp.einsum("pse,de->psd", grad_mods_img, w_mod, precision=exact_mode) + jnp.einsum(
        "pse,de->psd", grad_fmods_img, w_fmod, precision=exact_mode
    )
    grad_cond_part = jax.vjp(jax.nn.silu, cond_slots)[1](grad_act)[0]
    grad_cond = lax.psum(grad_cond_part, ("row", "col"))
    summed = lax.psum(
        (
            grad_w_patch,
            grad_b_patch,
            grad_w_mod,
            grad_b_mod,
            grad_w_qkv,
            grad_b_query,
            grad_b_value,
            grad_w_proj,
            grad_b_proj,
            grad_w_fc1,
            grad_b_fc1,
            grad_w_fc2,
            grad_b_fc2,
            grad_w_fmod,
            grad_b_fmod,
            grad_w_out,
            grad_b_out,
        ),
        ("batch", "row", "col"),
    )
    return (result_cols[None, None, None], grad_patch_cols[None, None, None], grad_cond) + tuple(
        summed
    )


def solution(mesh):
    placed = (
        P("batch", "row", "col", None, None),
        P("batch", None, None),
        P("batch", None, None),
        P("batch", "row", "col", None, None),
        P(),
        P(),
        P(),
        P(),
        P(),
        P(),
        P(),
        P(),
        P(),
        P(),
        P(),
        P(),
        P(),
        P(),
        P(),
        P(),
        P(),
    )
    return jax.shard_map(
        body,
        mesh=mesh,
        in_specs=placed,
        out_specs=(
            P("batch", "row", "col", None, None),
            P("batch", "row", "col", None, None),
            P("batch", None, None),
            P(),
            P(),
            P(),
            P(),
            P(),
            P(),
            P(),
            P(),
            P(),
            P(),
            P(),
            P(),
            P(),
            P(),
            P(),
            P(),
            P(),
        ),
        check_vma=False,
    )
```

profile of v0, /device:TPU:0, one launch (start us, length us, event | category | flops | bytes accessed | tf_op | source)
XLA Modules:
  0.0 549.7 jit_solution(18087392643285568274)
XLA Ops:
  7.8 1.0 and_select_fusion.3
  8.9 1.2 fusion.71
  10.2 0.8 select_reduce_fusion
  11.1 1.6 multiply_sine_fusion.1
  12.7 1.4 fusion.89
  14.4 1.7 convolution_add_fusion
  16.1 1.1 fusion.47
  18.8 1.0 copy-done.17
  19.7 10.5 %all-gather.1 = bf16[1024,384]{1,0:T(8,128)(2,1)} all-gather(bf16[256,384]{1,0:T(8,128)(2,1)S(1)} %slice.109), channel_id=3, replica_groups=mesh['batch'=8,'row'=2,'col'=2] {'row','col'}, dimensions={0}, use_global_device_ids=true | all-gather | bytes 983040 | tf_op jit(solution)/shard_map/all_gather | solution.py:235
  30.3 2.3 copy.55
  32.5 1.9 fusion.35
  34.5 1.7 copy.54
  36.4 2.6 fusion.90
  39.0 1.4 fusion
  40.5 1.2 copy-done.1
  42.3 9.3 %all-gather = bf16[1024,384]{1,0:T(8,128)(2,1)} all-gather(bf16[256,384]{1,0:T(8,128)(2,1)S(1)} %copy-done.40), channel_id=2, replica_groups=mesh['batch'=8,'row'=2,'col'=2] {'row','col'}, dimensions={0}, use_global_device_ids=true | all-gather | bytes 983040 | tf_op jit(solution)/shard_map/all_gather | solution.py:236
  51.6 2.3 copy.53
  53.9 4.4 fusion.14
  58.4 1.1 fusion.88
  60.9 1.1 copy-done.26
  62.0 1.5 fusion.87
  65.6 1.7 convert_reduce_fusion.1
  67.3 2.3 convert_reduce_fusion
  70.4 1.6 convert_reduce_fusion.2
  72.7 1.0 convolution_convert_fusion
  73.7 1.7 copy.56
  75.4 5.0 multiply_reduce_fusion
  80.5 1.4 multiply_convert_fusion
  81.9 2.3 convolution_multiply_fusion
  84.2 5.2 fusion.2
  89.8 4.0 convert_reduce_fusion.4
  94.5 1.5 convert_reduce_fusion.5
  95.9 2.1 fusion.92
  98.1 1.7 fusion.52
  99.8 2.1 fusion.94
  101.9 2.2 fusion.62
  104.1 1.9 fusion.95
  106.0 2.1 fusion.85
  108.1 5.1 reduce-scatter.3.cloned.1.call-done
  113.2 1.7 convert_bitcast_fusion.1
  114.9 29.5 %reduce-scatter.5.cloned.1.call-done = f32[1,256,384]{1,2,0:T(8,128)} async-done(((f32[1,1024,384]{1,2,0:T(8,128)}), f32[1,256,384]{1,2,0:T(8,128)}) %reduce-scatter.5.cloned.1.call-update) | async-done | bytes 393232 | tf_op jit(solution)/shard_map/reduce_scatter | solution.py:304
  144.4 1.7 convert_reduce_fusion.3
  146.1 2.6 fusion.84
  148.8 1.9 fusion.86
  151.0 0.9 copy-done.21
  152.0 1.6 fusion.91
  153.6 4.8 fusion.64
  158.4 0.9 convolution_bitcast_fusion
  159.7 2.9 fusion.42
  163.2 1.7 fusion.15
  165.0 2.4 fusion.93
  167.3 3.8 fusion.61
  171.1 6.5 %psum.126 = f32[1,4,384]{2,1,0:T(4,128)} all-reduce(f32[1,4,384]{2,1,0:T(4,128)S(1)} %fusion.61), channel_id=1, replica_groups=mesh['batch'=8,'row'=2,'col'=2] {'row','col'}, use_global_device_ids=true, to_apply=%region_21.22 | all-reduce | flops 1536 | bytes 12288 | tf_op jit(solution)/shard_map/psum | solution.py:364
  177.6 2.0 convolution_bitcast_fusion.1
  179.7 109.1 %all-reduce.5.cloned.1.call-done = (f32[16,384]{1,0:T(8,128)}, f32[384]{0:T(512)}, f32[2304]{0:T(1024)}, f32[384]{0:T(512)}, f32[384]{0:T(512)}, /*index=5*/f32[...) async-done(((f32[16,384]{1,0:T(8,128)}, f32[384]{0:T(512)}, f32[2304]{0:T(1024)}, f32[384]{0:T(512)}, ...) | async-done | bytes 99984 | tf_op jit(solution)/shard_map/psum | solution.py:365
  288.7 235.9 %all-reduce.7.cloned.1.call-done = (f32[384,2304]{1,0:T(8,128)}, f32[384,1152]{1,0:T(8,128)}, f32[384,384]{1,0:T(8,128)}, f32[384,1536]{1,0:T(8,128)}, f32[1536,384]{1,0:T(8,128)}, /*index=5*/f32[384,768]{1,0:T(8,128)}) async-done(((f32[384,2304]{1,0:T(8,128)}, f32[384,1152]{1,0:T(8,128)}, f32[384,384]{1,0:T(8,128)}, f32[384,1536]{1,0:T(8,128)}, f32[1536,384]{1,0:T(8,128)}, ...) | async-done | bytes 11796496 | tf_op jit(solution)/shard_map/psum | solution.py:365
  524.6 1.3 copy.80
  526.0 1.3 copy.81
  527.2 4.2 copy.82
  532.0 1.2 copy.84
  534.4 0.8 copy.87
  535.8 1.4 copy.89
  538.3 1.4 copy.91
  540.5 1.0 copy.93
  (210 shorter events, 16.9 us)
Async XLA Ops:
  7.2 7.2 %copy-start = (f32[384,2304]{1,0:T(8,128)S(1)}, f32[384,2304]{1,0:T(8,128)}, u32[]{:S(2)}) copy-start(f32[384,2304]{1,0:T(8,128)} %param.27) | copy-start | bytes 10616836
  7.2 7.2 %copy-start.47 = (f32[1,4,384]{2,1,0:T(4,128)S(1)}, f32[1,4,384]{2,1,0:T(4,128)}, u32[]{:S(2)}) copy-start(f32[1,4,384]{2,1,0:T(4,128)} %param.22) | copy-start | bytes 18436
  7.2 106.0 %reduce-scatter.3.cloned.1.call-start = ((), (), s32[]{:S(2)}) async-start(), calls=%async_computation.2 | async-start | bytes 1966080 | tf_op jit(solution)/shard_map/reduce_scatter | solution.py:303
  10.2 26.0 %copy-start.51 = (s32[256]{0:T(256)}, s32[256]{0:T(256)S(1)}, u32[]{:S(2)}) copy-start(s32[256]{0:T(256)S(1)} %convert_reduce_fusion.6) | copy-start | bytes 3076
  10.2 4.2 copy-start.65
  14.1 3.1 copy-start.7
  14.2 3.1 copy-start.58
  14.4 2.9 copy-start.62
  39.0 2.7 copy-start.1
  39.0 2.7 copy-start.49
  39.0 3.3 copy-start.40
  53.9 4.5 copy-start.4
  53.9 4.5 copy-start.8
  53.9 4.5 copy-start.25
  53.9 4.5 copy-start.70
  58.4 1.8 copy-start.10
  58.4 1.8 copy-start.66
  59.5 10.9 %copy-start.5 = (f32[256,384]{1,0:T(8,128)}, f32[256,384]{1,0:T(8,128)S(1)}, u32[]{:S(2)}) copy-start(f32[256,384]{1,0:T(8,128)S(1)} %get-tuple-element.115) | copy-start | bytes 1179652
  59.5 10.9 %copy-start.55 = (f32[256]{0:T(256)}, f32[256]{0:T(256)S(1)}, u32[]{:S(2)}) copy-start(f32[256]{0:T(256)S(1)} %broadcast_multiply_fusion.7) | copy-start | bytes 3076
  59.7 10.7 %copy-start.60 = (f32[256]{0:T(256)}, f32[256]{0:T(256)S(1)}, u32[]{:S(2)}) copy-start(f32[256]{0:T(256)S(1)} %add_rsqrt_fusion.1) | copy-start | bytes 3076
  60.2 1.7 copy-start.26
  60.2 1.7 copy-start.71
  62.0 5.3 copy-start.12
  62.0 2.0 copy-start.16
  62.0 2.0 copy-start.68
  62.0 2.6 copy-start.52
  67.2 2.3 copy-start.45
  67.2 3.2 copy-start.20
  75.4 5.0 slice-start
  75.4 5.0 slice-start.1
  81.9 2.3 copy-start.2
  84.2 60.2 %reduce-scatter.5.cloned.1.call-start = ((), (), s32[]{:S(2)}) async-start(), calls=%async_computation.3 | async-start | bytes 1966080 | tf_op jit(solution)/shard_map/reduce_scatter | solution.py:304
  89.5 6.4 %copy-start.53 = (s32[256]{0:T(256)S(1)}, s32[256]{0:T(256)}, u32[]{:S(2)}) copy-start(s32[256]{0:T(256)} %copy-done.51) | copy-start | bytes 3076
  89.5 199.3 %all-reduce.5.cloned.1.call-start = ((), (), s32[]{:S(2)}) async-start(), calls=%async_computation.4 | async-start | bytes 218112 | tf_op jit(solution)/shard_map/psum | solution.py:365
  94.5 9.6 %copy-start.24 = (bf16[256,1536]{1,0:T(8,128)(2,1)S(1)}, bf16[256,1536]{1,0:T(8,128)(2,1)}, u32[]{:S(2)}) copy-start(bf16[256,1536]{1,0:T(8,128)(2,1)} %copy-done.23) | copy-start | bytes 2359300
  94.5 9.6 %copy-start.31 = (bf16[256,384]{1,0:T(8,128)(2,1)S(1)}, bf16[256,384]{1,0:T(8,128)(2,1)}, u32[]{:S(2)}) copy-start(bf16[256,384]{1,0:T(8,128)(2,1)} %copy-done.30) | copy-start | bytes 589828
  98.1 3.8 copy-start.48
  104.1 1.9 copy-start.13
  104.1 1.9 copy-start.46
  106.0 40.1 %copy-start.59 = (f32[256]{0:T(256)S(1)}, f32[256]{0:T(256)}, u32[]{:S(2)}) copy-start(f32[256]{0:T(256)} %copy-done.58) | copy-start | bytes 3076
  146.1 2.6 copy-start.29
  146.1 2.7 copy-start.9
  146.1 2.7 copy-start.22
  146.1 2.7 copy-start.63
  148.7 2.0 copy-start.37
  148.8 2.0 copy-start.15
  148.8 2.0 copy-start.6
  148.8 2.0 copy-start.56
  148.8 2.0 copy-start.61
  150.7 7.7 %copy-start.19 = (f32[256,384]{1,0:T(8,128)}, f32[256,384]{1,0:T(8,128)S(1)}, u32[]{:S(2)}) copy-start(f32[256,384]{1,0:T(8,128)S(1)} %get-tuple-element.111) | copy-start | bytes 1179652
  153.6 4.8 copy-start.42
  153.6 4.8 copy-start.50
  159.4 365.2 %all-reduce.7.cloned.1.call-start = ((), (), s32[]{:S(2)}) async-start(), calls=%async_computation.5 | async-start | bytes 23592960 | tf_op jit(solution)/shard_map/psum | solution.py:365
  527.2 4.2 copy-start.64
  527.2 4.8 copy-start.33
  532.0 1.8 copy-start.74
  532.0 2.4 copy-start.41
  532.0 3.2 copy-start.73
  532.0 3.8 copy-start.28
  535.8 2.5 copy-start.27
  538.3 2.1 copy-start.38
  539.7 1.7 copy-start.69
  539.7 2.3 copy-start.54
  539.7 2.9 copy-start.77
  (20 other events, 24.6 us)
Sparse Core Ops, SparseCore 0:
  84.3 28.8 reduce-scatter.2
  116.3 28.0 reduce-scatter.4
  159.5 129.2 all-reduce.4
  296.7 227.8 all-reduce.6
where the time goes:
time: 551 us; the launch traced here: 550 us
  waiting for transfers between devices  380 us (69%)
  matrix products  71.8 us (13%)
  local copies, waits for them, and re-layouts  35.3 us (6%)
  blocking collectives  26.3 us (5%)
  other arithmetic  21.6 us (4%)
  between operations  14.5 us (3%)
    psum x2, waiting for transfers between devices, body(): lax.psum((grad_w_patch, grad_b_patch, grad_w_mod, grad_b_mod, grad_w_qkv,...  345 us
    reduce_scatter x1, waiting for transfers between devices, body(): lax.psum_scatter(grad_values_all, ('row', 'col'), scatter_dimension=1, ti...  29.5 us
    unnamed x180, local copies, waits for them, and re-layouts  26.6 us
  transfers between devices with their start and end apart: 4, of which 4 were waited for; matrix products, arithmetic and copies ran while one was open for 7% of the time, Pallas kernels for 0%

commit v1 on v0

v1 whole, which is shorter than its diff:
```python
import math

import jax
import jax.numpy as jnp
from jax import lax
from jax.experimental import pallas as pl
from jax.experimental.pallas import tpu as pltpu
from jax.sharding import PartitionSpec as P

HEADS = 6
HEAD_DIM = 64
BIG_SIDE = 16
SMALL_SIDE = 8
BIG_LEN = 1024
W = 384
T = 256
ALL = 1024
FF = 1536
PATCH = 16
OUTC = 32
BLOCKS = 4
BLOCK = T // BLOCKS
SMALL_AT = 1536
SLOT_AT = 1600
SLOT_ROWS = 48

exact_mode = lax.Precision.HIGHEST
eps_norm = 1e-06
low = jnp.bfloat16
full = jnp.float32


def mm(left_op, right_op, precision=None):
    return lax.dot_general(
        left_op,
        right_op,
        (((1,), (0,)), ((), ())),
        precision=precision,
        preferred_element_type=full,
    )


def mm_last(left_op, right_op, precision=None):
    return lax.dot_general(
        left_op,
        right_op,
        (((1,), (1,)), ((), ())),
        precision=precision,
        preferred_element_type=full,
    )


def mm_rows(left_op, right_op):
    return lax.dot_general(
        left_op, right_op, (((0,), (0,)), ((), ())), preferred_element_type=full
    )


def norm_stats(values):
    center = values - jnp.mean(values, axis=1, keepdims=True)
    inv_std = lax.rsqrt(jnp.mean(center * center, axis=1, keepdims=True) + eps_norm)
    return (center * inv_std, inv_std)


def norm_back(grad_in, normed, inv_std):
    return inv_std * (
        grad_in
        - jnp.mean(grad_in, axis=1, keepdims=True)
        - normed * jnp.mean(grad_in * normed, axis=1, keepdims=True)
    )


def per_token(mods, index):
    rows = mods[:, index * W : (index + 1) * W]
    return jnp.concatenate(
        [jnp.broadcast_to(rows[b : b + 1], (BLOCK, W)) for b in range(BLOCKS)], axis=0
    )


def block_sums(values):
    return jnp.concatenate(
        [
            jnp.sum(values[b * BLOCK : (b + 1) * BLOCK], axis=0, keepdims=True)
            for b in range(BLOCKS)
        ],
        axis=0,
    )


def same_image(big, rows, cols):
    row_seg = (lax.broadcasted_iota(jnp.int32, (rows, cols), 0) & (T - 1)) >> 6
    col_seg = (lax.broadcasted_iota(jnp.int32, (rows, cols), 1) & (T - 1)) >> 6
    gap = jnp.where(big, 0, row_seg - col_seg)
    return gap == 0


def gelu_parts(u):
    c = 0.7978845608028654
    square = u * u
    t = jnp.tanh(c * (u + 0.044715 * u * square))
    value = 0.5 * u * (1.0 + t)
    slope = 0.5 * (1.0 + t) + 0.5 * u * (1.0 - t * t) * (c * (1.0 + 3.0 * 0.044715 * square))
    return value, slope


def pair_half(rows, half):
    lane = lax.broadcasted_iota(jnp.int32, (rows, 2 * HEAD_DIM), 1)
    return (lane < HEAD_DIM) if half == 0 else (lane >= HEAD_DIM)


def front_kernel(
    meta,
    patches_all,
    cot,
    mods_ref,
    w_embed,
    b_patch,
    b_query,
    b_value,
    b_proj,
    b_fc1,
    b_fc2,
    w_out_t,
    b_out,
    w_qkv_hbm,
    w_proj_hbm,
    w_fc1_hbm,
    w_fc2_hbm,
    result,
    payload,
    qkv_all,
    entry_own,
    normed_own,
    inv_own,
    attended_out,
    grad_attn_out,
    grad_mid_out,
    activ_out,
    grad_mlp_out,
    entry_two_out,
    grad_inner_out,
    small_out,
    slots_out,
    w_qkv_low,
    w_qkv_v,
    w_proj_v,
    w_fc1_v,
    w_fc2_v,
    entry_all,
    mixed_ref,
    stat_ref,
    inner_ref,
    sems,
):
    copies = [
        pltpu.make_async_copy(src, dst, sems.at[at])
        for at, (src, dst) in enumerate(
            (
                (w_qkv_hbm, w_qkv_v),
                (w_proj_hbm, w_proj_v),
                (w_fc1_hbm, w_fc1_v),
                (w_fc2_hbm, w_fc2_v),
            )
        )
    ]
    for copy in copies:
        copy.start()
    big = meta[0] == 1
    tile_row = meta[1]
    tile_col = meta[2]
    token = lax.broadcasted_iota(jnp.int32, (32, ALL), 1)
    tile = token >> 8
    place = token & (T - 1)
    inside = place & 63
    row_here = tile_row ^ (tile & 1)
    col_here = tile_col ^ (tile >> 1)
    grid_row = jnp.where(
        big, row_here * BIG_SIDE + (place >> 4), row_here * SMALL_SIDE + (inside >> 3)
    )
    grid_col = jnp.where(
        big, col_here * BIG_SIDE + (place & 15), col_here * SMALL_SIDE + (inside & 7)
    )
    level = lax.broadcasted_iota(jnp.int32, (32, ALL), 0)
    stacked = jnp.concatenate(
        [
            patches_all[...],
            jnp.where(level == grid_row, 1.0, 0.0),
            jnp.where(level == grid_col, 1.0, 0.0),
        ],
        axis=0,
    )
    hidden_all = mm(stacked.T, w_embed[...], exact_mode) + b_patch[...]
    mods = mods_ref[...]
    shift_a = per_token(mods, 0)
    scale_a = 1.0 + per_token(mods, 1)
    hidden_in = hidden_all[:T]
    for tile_at in range(ALL // T):
        rows = slice(tile_at * T, (tile_at + 1) * T)
        normed, inv_std = norm_stats(hidden_all[rows])
        entry = (normed * scale_a + shift_a).astype(low)
        entry_all[rows] = entry
        if tile_at == 0:
            normed_own[...] = normed
            inv_own[...] = inv_std
            entry_own[...] = entry
    copies[0].wait()
    w_qkv_low[...] = w_qkv_v[...].astype(low)
    entries = entry_all[...]
    qkv_all[:, :W] = (mm(entries, w_qkv_low[:, :W]) + b_query[...]).astype(low)
    qkv_all[:, W : 2 * W] = mm(entries, w_qkv_low[:, W : 2 * W]).astype(low)
    qkv_all[:, 2 * W :] = (mm(entries, w_qkv_low[:, 2 * W :]) + b_value[...]).astype(low)
    allowed = same_image(big, T, ALL)
    lane = lax.broadcasted_iota(jnp.int32, (T, 2 * HEAD_DIM), 1)
    stat = jnp.zeros((T, 2 * HEAD_DIM), full)
    for pair in range(HEADS // 2):
        cols = slice(pair * 2 * HEAD_DIM, (pair + 1) * 2 * HEAD_DIM)
        q_pair = qkv_all[:T, cols] * low(1.0 / math.sqrt(HEAD_DIM))
        k_pair = qkv_all[:, W + cols.start : W + cols.stop]
        v_pair = qkv_all[:, 2 * W + cols.start : 2 * W + cols.stop]
        mixed = []
        for half in range(2):
            q_head = jnp.where(pair_half(T, half), q_pair, low(0.0))
            scores = jnp.where(allowed, mm_last(q_head, k_pair), -1e30)
            row_top = jnp.max(scores, axis=1, keepdims=True)
            exp_scores = jnp.exp(scores - row_top)
            row_total = jnp.sum(exp_scores, axis=1, keepdims=True)
            probs = (exp_scores * (1.0 / row_total)).astype(low)
            mixed.append(mm(probs, v_pair))
            stat = jnp.where(lane == 2 * pair + half, row_top + jnp.log(row_total), stat)
        mixed_ref[:, cols] = jnp.where(pair_half(T, 0), mixed[0], mixed[1])
    attended = mixed_ref[...].astype(low)
    attended_out[...] = attended
    copies[1].wait()
    w_proj_low = w_proj_v[...].astype(low)
    attn_out = mm(attended, w_proj_low) + b_proj[...]
    gate_a = per_token(mods, 2)
    hidden_mid = hidden_in + gate_a * attn_out
    normed_two, inv_two = norm_stats(hidden_mid)
    scale_m = 1.0 + per_token(mods, 4)
    entry_two = (normed_two * scale_m + per_token(mods, 3)).astype(low)
    entry_two_out[...] = entry_two
    copies[2].wait()
    w_fc1_low = w_fc1_v[...].astype(low)
    inner = mm(entry_two, w_fc1_low) + b_fc1[...]
    activ, slope = gelu_parts(inner)
    inner_ref[...] = slope
    activ_low = activ.astype(low)
    activ_out[...] = activ_low
    copies[3].wait()
    w_fc2_low = w_fc2_v[...].astype(low)
    mlp_out = mm(activ_low, w_fc2_low) + b_fc2[...]
    gate_m = per_token(mods, 5)
    hidden_out = hidden_mid + gate_m * mlp_out
    normed_three, inv_three = norm_stats(hidden_out)
    scale_f = 1.0 + per_token(mods, 7)
    entry_three = (normed_three * scale_f + per_token(mods, 6)).astype(low)
    w_out_low = w_out_t[...].astype(low)
    result[...] = mm_last(w_out_low, entry_three) + b_out[...]
    grad_out = cot[...].astype(low)
    small_out[...] = jnp.zeros_like(small_out)
    small_out[PATCH : PATCH + OUTC] = mm(grad_out, entry_three)
    at = PATCH + OUTC
    grad_out_tall = cot[...].T.astype(low)
    grad_b_out = jnp.sum(grad_out_tall.astype(full), axis=0, keepdims=True)
    small_out[at + 9 : at + 10, :OUTC] = grad_b_out
    grad_entry_three = mm(grad_out_tall, w_out_low)
    slots_out[24:28] = block_sums(grad_entry_three)
    slots_out[28:32] = block_sums(grad_entry_three * normed_three)
    grad_hidden_out = norm_back(grad_entry_three * scale_f, normed_three, inv_three)
    grad_mlp = (gate_m * grad_hidden_out).astype(low)
    grad_mlp_out[...] = grad_mlp
    slots_out[20:24] = block_sums(grad_hidden_out * mlp_out)
    small_out[at + 8 : at + 9] = jnp.sum(grad_mlp.astype(full), axis=0, keepdims=True)
    grad_activ = mm_last(grad_mlp, w_fc2_low)
    grad_inner = (grad_activ * inner_ref[...]).astype(low)
    grad_inner_out[...] = grad_inner
    grad_b_fc1 = jnp.sum(grad_inner.astype(full), axis=0, keepdims=True)
    for slab in range(FF // W):
        small_out[at + 4 + slab : at + 5 + slab] = grad_b_fc1[:, slab * W : (slab + 1) * W]
    grad_entry_two = mm_last(grad_inner, w_fc1_low)
    slots_out[12:16] = block_sums(grad_entry_two)
    slots_out[16:20] = block_sums(grad_entry_two * normed_two)
    grad_hidden_mid = grad_hidden_out + norm_back(grad_entry_two * scale_m, normed_two, inv_two)
    grad_mid_out[...] = grad_hidden_mid
    grad_attn = (gate_a * grad_hidden_mid).astype(low)
    grad_attn_out[...] = grad_attn
    slots_out[0:8] = jnp.zeros((8, W), full)
    slots_out[8:12] = block_sums(grad_hidden_mid * attn_out)
    small_out[at + 3 : at + 4] = jnp.sum(grad_attn.astype(full), axis=0, keepdims=True)
    grad_attended = mm_last(grad_attn, w_proj_low).astype(low)
    payload[:, :W] = grad_attended
    for pair in range(HEADS // 2):
        cols = slice(pair * 2 * HEAD_DIM, (pair + 1) * 2 * HEAD_DIM)
        product = grad_attended[:, cols].astype(full) * mixed_ref[:, cols]
        for half in range(2):
            picked = jnp.where(pair_half(T, half), product, 0.0)
            stat = jnp.where(
                lane == 8 + 2 * pair + half, jnp.sum(picked, axis=1, keepdims=True), stat
            )
    stat_ref[...] = stat
    first = stat.astype(low).astype(full)
    rest = stat - first
    second = rest.astype(low).astype(full)
    third = rest - second
    payload[:, W:] = (first + pltpu.roll(second, 16, 1) + pltpu.roll(third, 32, 1)).astype(low)


def query_kernel(
    meta,
    qkv_all,
    payload,
    stat_ref,
    activ,
    grad_mlp,
    entry_two,
    grad_inner,
    grad_query_out,
    grad_fc2,
    grad_fc1,
):
    big = meta[0] == 1
    allowed = same_image(big, T, ALL)
    for pair in range(HEADS // 2):
        cols = slice(pair * 2 * HEAD_DIM, (pair + 1) * 2 * HEAD_DIM)
        q_pair = qkv_all[:T, cols] * low(1.0 / math.sqrt(HEAD_DIM))
        k_pair = qkv_all[:, W + cols.start : W + cols.stop]
        v_pair = qkv_all[:, 2 * W + cols.start : 2 * W + cols.stop]
        do_pair = payload[:, cols]
        grads = []
        for half in range(2):
            head = 2 * pair + half
            q_head = jnp.where(pair_half(T, half), q_pair, low(0.0))
            do_head = jnp.where(pair_half(T, half), do_pair, low(0.0))
            scores = jnp.where(allowed, mm_last(q_head, k_pair), -1e30)
            probs = jnp.exp(scores - stat_ref[:, head : head + 1])
            grad_probs = mm_last(do_head, v_pair)
            grad_scores = (probs * (grad_probs - stat_ref[:, 8 + head : 9 + head])).astype(low)
            grads.append(mm(grad_scores, k_pair))
        grad_query_out[:, cols] = (
            jnp.where(pair_half(T, 0), grads[0], grads[1]) * (1.0 / math.sqrt(HEAD_DIM))
        ).astype(low)
    grad_fc2[...] = mm_rows(activ[...], grad_mlp[...]).astype(low)
    entry = entry_two[...]
    for slab in range(FF // W):
        grad_fc1[slab * W : (slab + 1) * W] = mm_rows(
            entry, grad_inner[:, slab * W : (slab + 1) * W]
        ).astype(low)


def key_kernel(
    meta,
    qkv_all,
    payload_all,
    grad_query,
    entry_own,
    normed_own,
    inv_own,
    attended,
    grad_attn,
    grad_mid,
    small,
    slots,
    mods_ref,
    act_ref,
    patches,
    w_patch,
    w_qkv_low,
    bundle,
    grad_patches,
    gk_ref,
    gv_ref,
):
    big = meta[0] == 1
    allowed = same_image(big, T, ALL)
    packed = payload_all[:, W:].astype(full)
    stat = packed + pltpu.roll(packed, 112, 1) + pltpu.roll(packed, 96, 1)
    stat_t = stat.T
    for pair in range(HEADS // 2):
        cols = slice(pair * 2 * HEAD_DIM, (pair + 1) * 2 * HEAD_DIM)
        q_pair = qkv_all[:, cols]
        k_pair = qkv_all[:T, W + cols.start : W + cols.stop] * low(1.0 / math.sqrt(HEAD_DIM))
        v_pair = qkv_all[:T, 2 * W + cols.start : 2 * W + cols.stop]
        do_pair = payload_all[:, cols]
        grad_k = []
        grad_v = []
        for half in range(2):
            head = 2 * pair + half
            k_head = jnp.where(pair_half(T, half), k_pair, low(0.0))
            v_head = jnp.where(pair_half(T, half), v_pair, low(0.0))
            scores = jnp.where(allowed, mm_last(k_head, q_pair), -1e30)
            probs = jnp.exp(scores - stat_t[head : head + 1])
            grad_probs = mm_last(v_head, do_pair)
            grad_scores = (probs * (grad_probs - stat_t[8 + head : 9 + head])).astype(low)
            grad_v.append(mm(probs.astype(low), do_pair))
            grad_k.append(mm(grad_scores, q_pair))
        gk_ref[:, cols] = (
            jnp.where(pair_half(T, 0), grad_k[0], grad_k[1]) * (1.0 / math.sqrt(HEAD_DIM))
        ).astype(low)
        gv_ref[:, cols] = jnp.where(pair_half(T, 0), grad_v[0], grad_v[1]).astype(low)
    entry = entry_own[...]
    grad_q = grad_query[...]
    grad_k = gk_ref[...]
    grad_v = gv_ref[...]
    bundle[:W] = mm_rows(entry, grad_q).astype(low)
    bundle[W : 2 * W] = mm_rows(entry, grad_k).astype(low)
    bundle[2 * W : 3 * W] = mm_rows(entry, grad_v).astype(low)
    bundle[3 * W : 4 * W] = mm_rows(attended[...], grad_attn[...]).astype(low)
    grad_entry = (
        mm_last(grad_q, w_qkv_low[:, :W])
        + mm_last(grad_k, w_qkv_low[:, W : 2 * W])
        + mm_last(grad_v, w_qkv_low[:, 2 * W :])
    )
    normed = normed_own[...]
    scale_a = 1.0 + per_token(mods_ref[...], 1)
    grad_in = grad_mid[...] + norm_back(grad_entry * scale_a, normed, inv_own[...])
    grad_patches[...] = mm_last(w_patch[...], grad_in, exact_mode)
    at = PATCH + OUTC
    line = lax.broadcasted_iota(jnp.int32, small.shape, 0)
    tail = small[...]
    tail = jnp.where(line == at, jnp.sum(grad_in, axis=0, keepdims=True), tail)
    tail = jnp.where(line == at + 1, jnp.sum(grad_q.astype(full), axis=0, keepdims=True), tail)
    tail = jnp.where(line == at + 2, jnp.sum(grad_v.astype(full), axis=0, keepdims=True), tail)
    grad_w_patch = mm(patches[...], grad_in, exact_mode)
    tail = jnp.concatenate([grad_w_patch, tail[PATCH:]], axis=0)
    bundle[SMALL_AT:SLOT_AT] = tail.astype(low)
    bundle[SLOT_AT:] = jnp.zeros((bundle.shape[0] - SLOT_AT, W), low)
    late = jnp.concatenate([block_sums(grad_entry), block_sums(grad_entry * normed)], axis=0)
    sums = jnp.concatenate([late, slots[8:]], axis=0)
    joined = []
    slot_line = lax.broadcasted_iota(jnp.int32, (BLOCKS, W), 0)
    for block in range(8):
        part = sums[4 * block : 4 * block + 4]
        whole = jnp.where(slot_line == 0, jnp.sum(part, axis=0, keepdims=True), 0.0)
        joined.append(jnp.where(big, whole, part))
    first_tile = (meta[1] == 0) & (meta[2] == 0)
    joined.append(jnp.where(first_tile, act_ref[...], 0.0))
    joined.append(jnp.zeros((SLOT_ROWS - 36, W), full))
    start = pl.multiple_of(SLOT_AT + meta[3] * SLOT_ROWS, 16)
    bundle[pl.ds(start, SLOT_ROWS)] = jnp.concatenate(joined, axis=0).astype(low)


def bit_swap(array, axis_name, bit):
    size = lax.axis_size(axis_name)
    return lax.ppermute(array, axis_name, [(i, i ^ (1 << bit)) for i in range(size)])


def bit_here(axis_name, bit):
    return (lax.axis_index(axis_name) >> bit) & 1


def join_halves(mine, other, axis_name, bit):
    low_side = bit_here(axis_name, bit) == 0
    return jnp.concatenate(
        [jnp.where(low_side, mine, other), jnp.where(low_side, other, mine)], axis=0
    )


def batch_bits():
    size = lax.axis_size("batch")
    assert size & (size - 1) == 0
    return size.bit_length() - 1


def halve_step(part, axis_name, bit):
    half = part.shape[0] // 2
    here = bit_here(axis_name, bit)
    keep = lax.dynamic_slice_in_dim(part, here * half, half, 0)
    send = lax.dynamic_slice_in_dim(part, (1 - here) * half, half, 0)
    got = bit_swap(send, axis_name, bit)
    return (keep.astype(jnp.float32) + got.astype(jnp.float32)).astype(jnp.bfloat16)


def colour_orders():
    bits = [("batch", bit) for bit in range(batch_bits())]
    first = ("col", 0)
    second = ("row", 0)
    return (
        [first, second] + bits,
        [first] + bits[:2] + [second] + bits[2:],
        [first] + bits[1:2] + [second] + bits[:1] + bits[2:],
    )


def sum_rows(parts):
    orders = colour_orders()
    depth = len(orders[0])
    for step in range(depth):
        parts = [halve_step(part, *order[step]) for part, order in zip(parts, orders)]
    for step in reversed(range(depth)):
        parts = [
            join_halves(part, bit_swap(part, *order[step]), *order[step])
            for part, order in zip(parts, orders)
        ]
    return parts


def shaped(*pairs):
    return [jax.ShapeDtypeStruct(shape, kind) for shape, kind in pairs]


vmem = pl.BlockSpec(memory_space=pltpu.VMEM)
smem = pl.BlockSpec(memory_space=pltpu.SMEM)
hbm = pl.BlockSpec(memory_space=pl.ANY)


def unslab(stacked, first, count):
    return jnp.concatenate(
        [stacked[(first + at) * W : (first + at + 1) * W] for at in range(count)], axis=1
    ).astype(full)


def position_table():
    quarter = W // 4
    rates = 1.0 / jnp.power(10000.0, jnp.arange(quarter, dtype=full) / quarter)
    angle = jnp.arange(32, dtype=full)[:, None] * rates[None, :]
    return jnp.concatenate([jnp.sin(angle), jnp.cos(angle)], axis=1)


def gather_tiles(array, axis):
    array = jnp.concatenate([array, bit_swap(array, "row", 0)], axis=axis)
    return jnp.concatenate([array, bit_swap(array, "col", 0)], axis=axis)


def body(
    patches,
    cond,
    image_lengths,
    cotangent,
    w_patch,
    b_patch,
    w_mod,
    b_mod,
    w_qkv,
    b_query,
    b_value,
    w_proj,
    b_proj,
    w_fc1,
    b_fc1,
    w_fc2,
    b_fc2,
    w_fmod,
    b_fmod,
    w_out,
    b_out,
):
    groups = lax.axis_size("batch")
    devices = groups * lax.axis_size("row") * lax.axis_size("col")
    slot_count = image_lengths.shape[2]
    patch_cols = patches[0, 0, 0]
    patches_all = gather_tiles(patch_cols, 1)
    big = image_lengths[0, 0, 0] == BIG_LEN
    group = lax.axis_index("batch")
    meta = jnp.stack(
        [big.astype(jnp.int32), lax.axis_index("row"), lax.axis_index("col"), group]
    ).astype(jnp.int32)
    act = jax.nn.silu(cond[0])
    mods = jnp.concatenate(
        [
            jnp.dot(act, w_mod, precision=exact_mode) + b_mod,
            jnp.dot(act, w_fmod, precision=exact_mode) + b_fmod,
        ],
        axis=1,
    )
    mods = jnp.where(big, mods[:1], mods)
    table = position_table()
    blank = jnp.zeros_like(table)
    w_embed = jnp.concatenate(
        [
            w_patch,
            jnp.concatenate([table, blank], axis=1),
            jnp.concatenate([blank, table], axis=1),
        ],
        axis=0,
    )
    (
        result,
        payload,
        qkv_all,
        entry_own,
        normed_own,
        inv_own,
        attended,
        grad_attn,
        grad_mid,
        activ,
        grad_mlp,
        entry_two,
        grad_inner,
        small,
        slots,
        w_qkv_low,
        stat,
    ) = pl.pallas_call(
        lambda *refs: front_kernel(
            *refs[:33], *refs[34:40], refs[33], *refs[40:]
        ),
        name="front",
        in_specs=[smem] + [vmem] * 12 + [hbm] * 4,
        out_specs=[vmem] * 17,
        out_shape=shaped(
            ((OUTC, T), full),
            ((T, W + 128), low),
            ((ALL, 3 * W), low),
            ((T, W), low),
            ((T, W), full),
            ((T, 1), full),
            ((T, W), low),
            ((T, W), low),
            ((T, W), full),
            ((T, FF), low),
            ((T, W), low),
            ((T, W), low),
            ((T, FF), low),
            ((64, W), full),
            ((32, W), full),
            ((W, 3 * W), low),
            ((T, 128), full),
        ),
        scratch_shapes=[
            pltpu.VMEM((W, 3 * W), full),
            pltpu.VMEM((W, W), full),
            pltpu.VMEM((W, FF), full),
            pltpu.VMEM((FF, W), full),
            pltpu.VMEM((ALL, W), low),
            pltpu.VMEM((T, W), full),
            pltpu.VMEM((T, FF), full),
            pltpu.SemaphoreType.DMA((4,)),
        ],
    )(
        meta,
        patches_all,
        cotangent[0, 0, 0],
        mods,
        w_embed,
        b_patch[None],
        b_query[None],
        b_value[None],
        b_proj[None],
        b_fc1[None],
        b_fc2[None],
        w_out.T,
        b_out[:, None],
        w_qkv,
        w_proj,
        w_fc1,
        w_fc2,
    )
    payload_all = gather_tiles(payload, 0)
    grad_query, grad_fc2, grad_fc1 = pl.pallas_call(
        query_kernel,
        name="query_side",
        in_specs=[smem] + [vmem] * 7,
        out_specs=[vmem] * 3,
        out_shape=shaped(((T, W), low), ((FF, W), low), ((FF, W), low)),
    )(meta, qkv_all, payload, stat, activ, grad_mlp, entry_two, grad_inner)
    unit = 16 * devices
    rows = -(-(SLOT_AT + groups * SLOT_ROWS) // unit) * unit
    bundle, grad_patch_cols = pl.pallas_call(
        key_kernel,
        name="key_side",
        in_specs=[smem] + [vmem] * 16,
        out_specs=[vmem] * 2,
        out_shape=shaped(((rows, W), low), ((PATCH, T), full)),
        scratch_shapes=[pltpu.VMEM((T, W), low), pltpu.VMEM((T, W), low)],
    )(
        meta,
        qkv_all,
        payload_all,
        grad_query,
        entry_own,
        normed_own,
        inv_own,
        attended,
        grad_attn,
        grad_mid,
        small,
        slots,
        mods,
        act,
        patch_cols,
        w_patch,
        w_qkv_low,
    )
    late, fc1_sum, fc2_sum = sum_rows([bundle, grad_fc1, grad_fc2])
    tail = late[SMALL_AT:SLOT_AT].astype(full)
    by_group = late[SLOT_AT : SLOT_AT + groups * SLOT_ROWS].reshape(groups, SLOT_ROWS, W)
    grad_slots_all = jnp.concatenate(
        [
            by_group[:, 4 * block : 4 * block + 4].reshape(groups * slot_count, W)
            for block in range(8)
        ],
        axis=1,
    )
    act_all = by_group[:, 32:36].reshape(groups * slot_count, W)
    grad_w_mods = lax.dot_general(
        act_all, grad_slots_all, (((0,), (0,)), ((), ())), preferred_element_type=full
    )
    grad_b_mods = jnp.sum(grad_slots_all.astype(full), axis=0)
    grad_slots = lax.dynamic_slice_in_dim(grad_slots_all, group * slot_count, slot_count, 0).astype(
        full
    )
    grad_act = lax.dot_general(
        grad_slots[:, : 6 * W], w_mod, (((1,), (1,)), ((), ())), precision=exact_mode
    ) + lax.dot_general(
        grad_slots[:, 6 * W :], w_fmod, (((1,), (1,)), ((), ())), precision=exact_mode
    )
    grad_cond = jax.vjp(jax.nn.silu, cond[0])[1](grad_act)[0][None]
    at = PATCH + OUTC
    summed = (
        tail[:PATCH],
        tail[at],
        grad_w_mods[:, : 6 * W],
        grad_b_mods[: 6 * W],
        unslab(late, 0, 3),
        tail[at + 1],
        tail[at + 2],
        unslab(late, 3, 1),
        tail[at + 3],
        unslab(fc1_sum, 0, FF // W),
        tail[at + 4 : at + 8].reshape(FF),
        fc2_sum.astype(full),
        tail[at + 8],
        grad_w_mods[:, 6 * W :],
        grad_b_mods[6 * W :],
        tail[PATCH:at].T,
        tail[at + 9, :OUTC],
    )
    return (result[None, None, None], grad_patch_cols[None, None, None], grad_cond) + tuple(
        summed
    )


def solution(mesh):
    placed = (
        P("batch", "row", "col", None, None),
        P("batch", None, None),
        P("batch", None, None),
        P("batch", "row", "col", None, None),
        P(),
        P(),
        P(),
        P(),
        P(),
        P(),
        P(),
        P(),
        P(),
        P(),
        P(),
        P(),
        P(),
        P(),
        P(),
        P(),
        P(),
    )
    return jax.shard_map(
        body,
        mesh=mesh,
        in_specs=placed,
        out_specs=(
            P("batch", "row", "col", None, None),
            P("batch", "row", "col", None, None),
            P("batch", None, None),
            P(),
            P(),
            P(),
            P(),
            P(),
            P(),
            P(),
            P(),
            P(),
            P(),
            P(),
            P(),
            P(),
            P(),
            P(),
            P(),
            P(),
        ),
        check_vma=False,
    )
```

time: 551 us -> 201 us (0.36)
  waiting for transfers between devices: 380 us -> 58.6 us
  matrix products: 71.8 us -> 10.4 us
  Pallas kernels: 0 us -> 33.5 us
  starting transfers between devices: 0.65 us -> 28.3 us
  blocking collectives: 26.3 us -> 0 us
  between operations: 14.5 us -> 1.9 us
  local copies, waits for them, and re-layouts: 35.3 us -> 43.7 us
    psum x2 -> x0, waiting for transfers between devices: 345 us -> none  [body(): lax.psum((grad_w_patch, grad_b_patch, grad_w_mod, grad_b_mod, grad_w_qkv,...]
    dot_general x34 -> x5, matrix products: 71.8 us -> 10.4 us  [the longest x1 2.59 us: body(): lax.dot_general(grad_slots[:, :6 * W], w_mod, (((1,), (1,)), ((), ())), p...]
    ppermute x0 -> x34, waiting for transfers between devices: none -> 58.6 us  [bit_swap(): lax.ppermute(array, axis_name, [(i, i ^ 1 << bit) for i in range(size)])]
    reduce_scatter x2 -> x0, waiting for transfers between devices: 34.6 us -> none  [the longest x1 29.5 us: body(): lax.psum_scatter(grad_values_all, ('row', 'col'), scatter_dimension=1, ti...]
    pallas_call x0 -> x3, Pallas kernels: none -> 33.5 us  [the longest x1 16.4 us: body(): pl.pallas_call(lambda *refs: front_kernel(*refs[:33], *refs[34:40], refs[...]
    ppermute x0 -> x34, starting transfers between devices: none -> 28.3 us  [bit_swap(): lax.ppermute(array, axis_name, [(i, i ^ 1 << bit) for i in range(size)])]
    unnamed x180 -> x41, local copies, waits for them, and re-layouts: 26.6 us -> 6.6 us
    all_gather x2 -> x0, blocking collectives: 19.9 us -> none  [the longest x1 10.5 us: body(): lax.all_gather(key_tiles, ('row', 'col'), axis=1, tiled=True)]
  transfers between devices with their start and end apart: 4 -> 34, of which waited for: 4 -> 18; matrix products, arithmetic and copies ran while one was open for 7% -> 17% of each run, Pallas kernels for 0% -> 5%
where the time goes in v1:
time: 201 us; the launch traced here: 199 us
  waiting for transfers between devices  58.6 us (29%)
  local copies, waits for them, and re-layouts  43.7 us (22%)
  Pallas kernels  33.5 us (17%)
  starting transfers between devices  28.3 us (14%)
  other arithmetic  22.6 us (11%)
  matrix products  10.4 us (5%)
    ppermute x34, waiting for transfers between devices, bit_swap(): lax.ppermute(array, axis_name, [(i, i ^ 1 << bit) for i in range(size)])  58.6 us
    ppermute x34, starting transfers between devices, bit_swap(): lax.ppermute(array, axis_name, [(i, i ^ 1 << bit) for i in range(size)])  28.3 us
    pallas_call x1, Pallas kernels, body(): pl.pallas_call(lambda *refs: front_kernel(*refs[:33], *refs[34:40], refs[...  16.4 us
    reshape x8, local copies, waits for them, and re-layouts, body(): by_group[:, 4 * block:4 * block + 4].reshape(groups * slot_count, W)  10.8 us
    pallas_call x1, Pallas kernels, body(): pl.pallas_call(key_kernel, name='key_side', in_specs=[smem] + [vmem] * 16...  9.73 us
    pallas_call x1, Pallas kernels, body(): pl.pallas_call(query_kernel, name='query_side', in_specs=[smem] + [vmem]...  7.36 us
    unnamed x41, local copies, waits for them, and re-layouts  6.6 us
    dynamic_slice x15, local copies, waits for them, and re-layouts, halve_step(): send = lax.dynamic_slice_in_dim(part, (1 - here) * half, half, 0)  5.95 us
  transfers between devices with their start and end apart: 34, of which 18 were waited for; matrix products, arithmetic and copies ran while one was open for 17% of the time, Pallas kernels for 5%

profile of v1, /device:TPU:0, one launch (start us, length us, event | category | flops | bytes accessed | tf_op | source)
XLA Modules:
  0.0 199.0 jit_solution(14477514483122451192)
XLA Ops:
  0.7 3.1 %collective-permute-start = (f32[16,256]{1,0:T(8,128)}, f32[16,256]{1,0:T(8,128)}, u32[]{:S(2)}, u32[]{:S(2)}) collective-permute-start(f32[16,256]{1,0:T(8,128)} %bitcast.46), channel_id=1, source_target_pairs={{0,2},{2,0},{1,3},{3,1},{4,6},{6,4},{5,7},{7,5},{8,10},{10,8},{9,1... | collective-permute-start | bytes 49160 | tf_op jit(solution)/shard_map/ppermute | solution.py:444
  4.5 1.9 convolution_add_fusion.1
  6.5 2.5 %convolution_add_fusion = f32[4,2304]{1,0:T(4,128)S(1)} fusion(f32[384,2304]{1,0:T(8,128)S(1)} %copy-done, f32[2304]{0:T(1024)} %param.28, f32[1,4,384]{2,1,0:T(4,128)} %param.22), kind=kOutput, calls=%fused_computation | convolution fusion | flops 42482688 | bytes 3591168 | tf_op jit(solution)/shard_map/dot_general | solution.py:560
  10.3 1.3 pad_maximum_fusion.17
  12.3 1.2 broadcast_in_dim.50.refs_5_
  13.5 1.2 broadcast_in_dim.51.refs_6_
  14.8 1.2 broadcast_in_dim.52.refs_7_
  16.0 1.2 broadcast_in_dim.53.refs_8_
  17.2 1.2 broadcast_in_dim.55.refs_10_
  18.5 1.3 broadcast_in_dim.54.refs_9_
  19.8 1.3 copy.41.refs_12_
  21.1 1.4 pad_maximum_fusion.15.refs_1_
  22.5 16.4 %front.1 = (f32[32,256]{1,0:T(8,128)}, bf16[256,512]{1,0:T(8,128)(2,1)}, bf16[1024,1152]{1,0:T(8,128)(2,1)}, bf16[256,384]{1,0:T(8,128)(2,1)}, f32[256,384]{1,0:...) custom-call(s32[4]{0:T(128)} %pad_add_fusion.refs_0_.meta, ...), custom_call_target="tpu_custom_call" | custom-call | tf_op jit(solution)/shard_map/front/pallas_call | solution.py:594
  38.9 7.4 %query_side.1 = (bf16[256,384]{1,0:T(8,128)(2,1)}, bf16[1536,384]{1,0:T(8,128)(2,1)}, bf16[1536,384]{1,0:T(8,128)(2,1)}) custom-call(s32[4]{0:T(128)} %pad_add_fusion.refs_0_.meta, bf16[1024,1152]{1,0:T(8,128)(2,1)} %get-tuple-element.43.qkv_all, bf16[256,512]{1,0:T(8,128)(2,1)} %get-tuple-element.44.payload, f32[256,128]{1,0:T(8,128)} %get-tuple-element.45.stat_ref, ...), custom_call_target="tpu_custom_call" | custom-call | tf_op jit(solution)/shard_map/query_side/pallas_call | solution.py:650
  46.3 2.0 %constant_dynamic-slice_fusion.4 = bf16[768,384]{1,0:T(8,128)(2,1)} fusion(bf16[1536,384]{1,0:T(8,128)(2,1)} %get-tuple-element.63, s32[]{:T(128)S(6)} %select_n.293), kind=kLoop, calls=%fused_computation.98 | loop fusion | bytes 1179652 | tf_op jit(solution)/shard_map/dynamic_slice | solution.py:468
  50.6 6.8 %collective-permute-done.2 = bf16[256,512]{1,0:T(8,128)(2,1)} collective-permute-done((bf16[256,512]{1,0:T(8,128)(2,1)}, bf16[256,512]{1,0:T(8,128)(2,1)}, u32[]{:S(2)}, u32[]{:S(2)}) %collective-permute-start.2) | collective-permute-done | bytes 262176 | tf_op jit(solution)/shard_map/ppermute | solution.py:444
  58.5 1.4 add_convert_fusion.1
  60.7 1.5 collective-permute-start.25
  62.3 1.2 add_convert_fusion.2
  65.0 1.5 collective-permute-start.15
  66.6 2.0 pad_maximum_fusion.payload_all
  68.6 9.7 %key_side.1 = (bf16[2048,384]{1,0:T(8,128)(2,1)}, f32[16,256]{1,0:T(8,128)}) custom-call(s32[4]{0:T(128)} %pad_add_fusion.refs_0_.meta, bf16[1024,1152]{1,0:T(8,128)(2,1)} %get-tuple-element.43.qkv_all, bf16[1024,512]{1,0:T(8,128)(2,1)} %pad_maximum_fusion.payload_all, bf16[256,384]{1,0:T(8,128)(2,1)} %get-tuple-element.50.grad_query, ...), custom_call_target="tpu_custom_call" | custom-call | tf_op jit(solution)/shard_map/key_side/pallas_call | solution.py:659
  78.3 1.3 constant_dynamic-slice_fusion.14
  83.3 3.8 %collective-permute-done.26 = bf16[192,384]{1,0:T(8,128)(2,1)S(1)} collective-permute-done((bf16[192,384]{1,0:T(8,128)(2,1)S(1)}, bf16[192,384]{1,0:T(8,128)(2,1)S(1)}, u32[]{:S(2)}, u32[]{:S(2)}) %collective-permute-start.26) | collective-permute-done | bytes 147488 | tf_op jit(solution)/shard_map/ppermute | solution.py:444
  88.9 1.2 collective-permute-start.17
  90.1 1.5 collective-permute-done.27
  91.6 2.6 %collective-permute-start.28 = (bf16[48,384]{1,0:T(8,128)(2,1)S(1)}, bf16[48,384]{1,0:T(8,128)(2,1)S(1)}, u32[]{:S(2)}, u32[]{:S(2)}) collective-permute-start(bf16[48,384]{1,0:T(8,128)(2,1)S(1)} %constant_dynamic-slice_fusion), channel_id=1, source_target_pairs={{0,16},{4,20},{8,24},{12,28},{16,0},{20,4},{24,8},{28,12},{1,17},{... | collective-permute-start | bytes 110600 | tf_op jit(solution)/shard_map/ppermute | solution.py:444
  94.3 1.7 collective-permute-start.18
  96.0 1.6 collective-permute-done.28
  97.6 1.6 collective-permute-start.29
  99.6 1.4 collective-permute-start.19
  100.9 1.6 collective-permute-done.29
  103.1 1.7 collective-permute-done.19
  105.8 1.2 collective-permute-done.30
  108.2 1.2 collective-permute-start.31
  110.4 5.9 %collective-permute-done.5 = bf16[512,384]{1,0:T(8,128)(2,1)S(1)} collective-permute-done((bf16[512,384]{1,0:T(8,128)(2,1)S(1)}, bf16[512,384]{1,0:T(8,128)(2,1)S(1)}, u32[]{:S(2)}, u32[]{:S(2)}) %collective-permute-start.5) | collective-permute-done | bytes 393248 | tf_op jit(solution)/shard_map/ppermute | solution.py:444
  117.0 1.7 collective-permute-start.22
  118.7 3.5 %collective-permute-done.6 = bf16[256,384]{1,0:T(8,128)(2,1)S(1)} collective-permute-done((bf16[256,384]{1,0:T(8,128)(2,1)S(1)}, bf16[256,384]{1,0:T(8,128)(2,1)S(1)}, u32[]{:S(2)}, u32[]{:S(2)}) %collective-permute-start.6) | collective-permute-done | bytes 196640 | tf_op jit(solution)/shard_map/ppermute | solution.py:444
  122.4 5.7 %collective-permute-done.7 = bf16[128,384]{1,0:T(8,128)(2,1)S(1)} collective-permute-done((bf16[128,384]{1,0:T(8,128)(2,1)S(1)}, bf16[128,384]{1,0:T(8,128)(2,1)S(1)}, u32[]{:S(2)}, u32[]{:S(2)}) %collective-permute-start.7) | collective-permute-done | bytes 98336 | tf_op jit(solution)/shard_map/ppermute | solution.py:444
  128.2 1.1 collective-permute-start.8
  130.3 3.2 %collective-permute-done.8 = bf16[64,384]{1,0:T(8,128)(2,1)S(1)} collective-permute-done((bf16[64,384]{1,0:T(8,128)(2,1)S(1)}, bf16[64,384]{1,0:T(8,128)(2,1)S(1)}, u32[]{:S(2)}, u32[]{:S(2)}) %collective-permute-start.8) | collective-permute-done | bytes 49184 | tf_op jit(solution)/shard_map/ppermute | solution.py:444
  134.5 4.1 %collective-permute-done.9 = bf16[64,384]{1,0:T(8,128)(2,1)S(1)} collective-permute-done((bf16[64,384]{1,0:T(8,128)(2,1)S(1)}, bf16[64,384]{1,0:T(8,128)(2,1)S(1)}, u32[]{:S(2)}, u32[]{:S(2)}) %collective-permute-start.9) | collective-permute-done | bytes 49184 | tf_op jit(solution)/shard_map/ppermute | solution.py:444
  138.9 4.4 %collective-permute-done.10 = bf16[128,384]{1,0:T(8,128)(2,1)S(1)} collective-permute-done((bf16[128,384]{1,0:T(8,128)(2,1)S(1)}, bf16[128,384]{1,0:T(8,128)(2,1)S(1)}, u32[]{:S(2)}, u32[]{:S(2)}) %collective-permute-start.10) | collective-permute-done | bytes 98336 | tf_op jit(solution)/shard_map/ppermute | solution.py:444
  144.2 5.0 %collective-permute-done.11 = bf16[256,384]{1,0:T(8,128)(2,1)S(1)} collective-permute-done((bf16[256,384]{1,0:T(8,128)(2,1)S(1)}, bf16[256,384]{1,0:T(8,128)(2,1)S(1)}, u32[]{:S(2)}, u32[]{:S(2)}) %collective-permute-start.11) | collective-permute-done | bytes 196640 | tf_op jit(solution)/shard_map/ppermute | solution.py:444
  150.5 6.6 %collective-permute-done.12 = bf16[512,384]{1,0:T(8,128)(2,1)S(1)} collective-permute-done((bf16[512,384]{1,0:T(8,128)(2,1)S(1)}, bf16[512,384]{1,0:T(8,128)(2,1)S(1)}, u32[]{:S(2)}, u32[]{:S(2)}) %collective-permute-start.12) | collective-permute-done | bytes 393248 | tf_op jit(solution)/shard_map/ppermute | solution.py:444
  157.7 1.6 maximum_convert_fusion.1
  159.2 1.7 maximum_convert_fusion
  160.9 1.2 broadcast_select_fusion
  166.1 1.3 reshape.93
  167.5 1.3 reshape.92
  168.8 1.3 reshape.91
  170.2 1.3 reshape.90
  171.5 1.3 reshape.89
  172.9 1.3 reshape.88
  174.2 1.3 reshape.87
  175.6 1.4 reshape.86
  176.9 1.4 reshape.85
  184.9 1.5 fusion.22
  187.6 2.1 %slice.159 = f32[384,2304]{1,0:T(8,128)} slice(f32[384,3072]{1,0:T(8,128)S(1)} %fusion.22), slice={[0:384], [0:2304]} | slice | bytes 7077888 | tf_op jit(solution)/shard_map/slice | solution.py:713
  190.2 1.1 fusion.18
  191.4 2.6 %fusion.3 = f32[4,384]{1,0:T(4,128)S(1)} fusion(f32[384,2304]{1,0:T(8,128)S(1)} %copy-done, bf16[32,3072]{1,0:T(8,128)(2,1)} %copy-done.13, s32[]{:T(128)S(6)} %select_n.285), kind=kOutput, calls=%fused_computation.78 | convolution fusion | flops 42467328 | bytes 3563524 | tf_op jit(solution)/shard_map/dot_general | solution.py:703
  193.9 1.3 slice.174
  195.3 1.3 fusion.1
  197.1 1.9 fusion.11
  (157 shorter events, 36.1 us)
Async XLA Ops:
  0.7 5.8 %copy-start = (f32[384,2304]{1,0:T(8,128)S(1)}, f32[384,2304]{1,0:T(8,128)}, u32[]{:S(2)}) copy-start(f32[384,2304]{1,0:T(8,128)} %param.27) | copy-start | bytes 10616836
  0.7 9.7 %collective-permute-start = (f32[16,256]{1,0:T(8,128)}, f32[16,256]{1,0:T(8,128)}, u32[]{:S(2)}, u32[]{:S(2)}) collective-permute-start(f32[16,256]{1,0:T(8,128)} %bitcast.46), channel_id=1, source_target_pairs={{0,2},{2,0},{1,3},{3,1},{4,6},{6,4},{5,7},{7,5},{8,10},{10,8},{9,1... | collective-permute-start | bytes 49160 | tf_op jit(solution)/shard_map/ppermute | solution.py:444
  6.4 3.2 %copy-start.15 = (f32[16,384]{1,0:T(8,128)S(1)}, f32[16,384]{1,0:T(8,128)}, u32[]{:S(2)}) copy-start(f32[16,384]{1,0:T(8,128)} %w_patch.1) | copy-start | bytes 73732
  6.4 3.9 %copy-start.14 = (f32[1,1,1,16,256]{4,3,2,1,0:T(8,128)S(1)}, f32[1,1,1,16,256]{4,3,2,1,0:T(8,128)}, u32[]{:S(2)}) copy-start(f32[1,1,1,16,256]{4,3,2,1,0:T(8,128)} %param.21) | copy-start | bytes 49156
  11.7 9.5 %collective-permute-start.1 = (f32[16,512]{1,0:T(8,128)}, f32[16,512]{1,0:T(8,128)}, u32[]{:S(2)}, u32[]{:S(2)}) collective-permute-start(f32[16,512]{1,0:T(8,128)} %pad_maximum_fusion.17), channel_id=1, source_target_pairs={{0,1},{1,0},{2,3},{3,2},{4,5},{5,4},{6,7},{7,6},{8,9},{9,8},{10,11... | collective-permute-start | bytes 98312 | tf_op jit(solution)/shard_map/ppermute | solution.py:444
  46.3 2.8 %copy-start.11 = (bf16[1536,384]{1,0:T(8,128)(2,1)S(1)}, bf16[1536,384]{1,0:T(8,128)(2,1)}, u32[]{:S(2)}) copy-start(bf16[1536,384]{1,0:T(8,128)(2,1)} %get-tuple-element.62) | copy-start | bytes 3538948
  46.3 3.7 %copy-start.16 = (f32[1,4,384]{2,1,0:T(4,128)S(1)}, f32[1,4,384]{2,1,0:T(4,128)}, u32[]{:S(2)}) copy-start(f32[1,4,384]{2,1,0:T(4,128)} %param.22) | copy-start | bytes 18436
  48.3 10.2 %collective-permute-start.24 = (bf16[768,384]{1,0:T(8,128)(2,1)}, bf16[768,384]{1,0:T(8,128)(2,1)}, u32[]{:S(2)}, u32[]{:S(2)}) collective-permute-start(bf16[768,384]{1,0:T(8,128)(2,1)} %constant_dynamic-slice_fusion.4), channel_id=1, source_target_pairs={{0,1},{1,0},{2,3},{3,2},{4,5},{5,4},{6,7},{7,6},{8,9},{9,8},{10,11... | collective-permute-start | bytes 1769480 | tf_op jit(solution)/shard_map/ppermute | solution.py:444
  48.8 8.5 %collective-permute-start.2 = (bf16[256,512]{1,0:T(8,128)(2,1)}, bf16[256,512]{1,0:T(8,128)(2,1)}, u32[]{:S(2)}, u32[]{:S(2)}) collective-permute-start(bf16[256,512]{1,0:T(8,128)(2,1)} %get-tuple-element.44.payload), channel_id=1, source_target_pairs={{0,2},{2,0},{1,3},{3,1},{4,6},{6,4},{5,7},{7,5},{8,10},{10,8},{9,1... | collective-permute-start | bytes 786440 | tf_op jit(solution)/shard_map/ppermute | solution.py:444
  49.9 12.3 %collective-permute-start.14 = (bf16[768,384]{1,0:T(8,128)(2,1)}, bf16[768,384]{1,0:T(8,128)(2,1)}, u32[]{:S(2)}, u32[]{:S(2)}) collective-permute-start(bf16[768,384]{1,0:T(8,128)(2,1)} %constant_dynamic-slice_fusion.9), channel_id=1, source_target_pairs={{0,1},{1,0},{2,3},{3,2},{4,5},{5,4},{6,7},{7,6},{8,9},{9,8},{10,11... | collective-permute-start | bytes 1769480 | tf_op jit(solution)/shard_map/ppermute | solution.py:444
  50.5 11.7 %copy-start.12 = (bf16[1536,384]{1,0:T(8,128)(2,1)S(1)}, bf16[1536,384]{1,0:T(8,128)(2,1)}, u32[]{:S(2)}) copy-start(bf16[1536,384]{1,0:T(8,128)(2,1)} %get-tuple-element.62) | copy-start | bytes 3538948
  58.4 8.1 %collective-permute-start.3 = (bf16[512,512]{1,0:T(8,128)(2,1)S(1)}, bf16[512,512]{1,0:T(8,128)(2,1)S(1)}, u32[]{:S(2)}, u32[]{:S(2)}) collective-permute-start(bf16[512,512]{1,0:T(8,128)(2,1)S(1)} %pad_maximum_fusion.5), channel_id=1, source_target_pairs={{0,1},{1,0},{2,3},{3,2},{4,5},{5,4},{6,7},{7,6},{8,9},{9,8},{10,11... | collective-permute-start | bytes 1572872 | tf_op jit(solution)/shard_map/ppermute | solution.py:444
  59.9 2.3 %copy-start.7 = (bf16[768,384]{1,0:T(8,128)(2,1)}, bf16[768,384]{1,0:T(8,128)(2,1)S(1)}, u32[]{:S(2)}) copy-start(bf16[768,384]{1,0:T(8,128)(2,1)S(1)} %add_convert_fusion.1) | copy-start | bytes 1769476
  59.9 6.6 %copy-start.9 = (bf16[256,512]{1,0:T(8,128)(2,1)S(1)}, bf16[256,512]{1,0:T(8,128)(2,1)}, u32[]{:S(2)}) copy-start(bf16[256,512]{1,0:T(8,128)(2,1)} %get-tuple-element.44.payload) | copy-start | bytes 786436
  60.7 19.0 %collective-permute-start.25 = (bf16[384,384]{1,0:T(8,128)(2,1)}, bf16[384,384]{1,0:T(8,128)(2,1)}, u32[]{:S(2)}, u32[]{:S(2)}) collective-permute-start(bf16[384,384]{1,0:T(8,128)(2,1)} %constant_dynamic-slice_fusion.3), channel_id=1, source_target_pairs={{0,8},{4,12},{8,0},{12,4},{16,24},{20,28},{24,16},{28,20},{1,9},{5... | collective-permute-start | bytes 884744 | tf_op jit(solution)/shard_map/ppermute | solution.py:444
  63.5 0.8 copy-start.5
  65.0 16.7 %collective-permute-start.15 = (bf16[384,384]{1,0:T(8,128)(2,1)}, bf16[384,384]{1,0:T(8,128)(2,1)}, u32[]{:S(2)}, u32[]{:S(2)}) collective-permute-start(bf16[384,384]{1,0:T(8,128)(2,1)} %constant_dynamic-slice_fusion.8), channel_id=1, source_target_pairs={{0,4},{4,0},{8,12},{12,8},{16,20},{20,16},{24,28},{28,24},{1,5},{5... | collective-permute-start | bytes 884744 | tf_op jit(solution)/shard_map/ppermute | solution.py:444
  78.3 1.4 copy-start.8
  78.3 3.4 %copy-start.6 = (bf16[768,384]{1,0:T(8,128)(2,1)S(1)}, bf16[768,384]{1,0:T(8,128)(2,1)}, u32[]{:S(2)}) copy-start(bf16[768,384]{1,0:T(8,128)(2,1)} %copy-done.5) | copy-start | bytes 1769476
  79.6 27.4 %collective-permute-start.4 = (bf16[1024,384]{1,0:T(8,128)(2,1)S(1)}, bf16[1024,384]{1,0:T(8,128)(2,1)S(1)}, u32[]{:S(2)}, u32[]{:S(2)}) collective-permute-start(bf16[1024,384]{1,0:T(8,128)(2,1)S(1)} %constant_dynamic-slice_fusion.14), channel_id=1, source_target_pairs={{0,1},{1,0},{2,3},{3,2},{4,5},{5,4},{6,7},{7,6},{8,9},{9,8},{10,11... | collective-permute-start | bytes 2359304 | tf_op jit(solution)/shard_map/ppermute | solution.py:444
  80.8 6.3 %collective-permute-start.26 = (bf16[192,384]{1,0:T(8,128)(2,1)S(1)}, bf16[192,384]{1,0:T(8,128)(2,1)S(1)}, u32[]{:S(2)}, u32[]{:S(2)}) collective-permute-start(bf16[192,384]{1,0:T(8,128)(2,1)S(1)} %constant_dynamic-slice_fusion.2), channel_id=1, source_target_pairs={{0,2},{2,0},{1,3},{3,1},{4,6},{6,4},{5,7},{7,5},{8,10},{10,8},{9,1... | collective-permute-start | bytes 442376 | tf_op jit(solution)/shard_map/ppermute | solution.py:444
  82.8 24.2 %copy-start.10 = (bf16[2048,384]{1,0:T(8,128)(2,1)S(1)}, bf16[2048,384]{1,0:T(8,128)(2,1)}, u32[]{:S(2)}) copy-start(bf16[2048,384]{1,0:T(8,128)(2,1)} %get-tuple-element.61) | copy-start | bytes 4718596
  82.8 6.0 %collective-permute-start.16 = (bf16[192,384]{1,0:T(8,128)(2,1)S(1)}, bf16[192,384]{1,0:T(8,128)(2,1)S(1)}, u32[]{:S(2)}, u32[]{:S(2)}) collective-permute-start(bf16[192,384]{1,0:T(8,128)(2,1)S(1)} %constant_dynamic-slice_fusion.7), channel_id=1, source_target_pairs={{0,8},{4,12},{8,0},{12,4},{16,24},{20,28},{24,16},{28,20},{1,9},{5... | collective-permute-start | bytes 442376 | tf_op jit(solution)/shard_map/ppermute | solution.py:444
  87.2 4.4 %collective-permute-start.27 = (bf16[96,384]{1,0:T(8,128)(2,1)S(1)}, bf16[96,384]{1,0:T(8,128)(2,1)S(1)}, u32[]{:S(2)}, u32[]{:S(2)}) collective-permute-start(bf16[96,384]{1,0:T(8,128)(2,1)S(1)} %constant_dynamic-slice_fusion.1), channel_id=1, source_target_pairs={{0,4},{4,0},{8,12},{12,8},{16,20},{20,16},{24,28},{28,24},{1,5},{5... | collective-permute-start | bytes 221192 | tf_op jit(solution)/shard_map/ppermute | solution.py:444
  88.9 5.4 %collective-permute-start.17 = (bf16[96,384]{1,0:T(8,128)(2,1)S(1)}, bf16[96,384]{1,0:T(8,128)(2,1)S(1)}, u32[]{:S(2)}, u32[]{:S(2)}) collective-permute-start(bf16[96,384]{1,0:T(8,128)(2,1)S(1)} %constant_dynamic-slice_fusion.6), channel_id=1, source_target_pairs={{0,2},{2,0},{1,3},{3,1},{4,6},{6,4},{5,7},{7,5},{8,10},{10,8},{9,1... | collective-permute-start | bytes 221192 | tf_op jit(solution)/shard_map/ppermute | solution.py:444
  91.6 5.9 %collective-permute-start.28 = (bf16[48,384]{1,0:T(8,128)(2,1)S(1)}, bf16[48,384]{1,0:T(8,128)(2,1)S(1)}, u32[]{:S(2)}, u32[]{:S(2)}) collective-permute-start(bf16[48,384]{1,0:T(8,128)(2,1)S(1)} %constant_dynamic-slice_fusion), channel_id=1, source_target_pairs={{0,16},{4,20},{8,24},{12,28},{16,0},{20,4},{24,8},{28,12},{1,17},{... | collective-permute-start | bytes 110600 | tf_op jit(solution)/shard_map/ppermute | solution.py:444
  94.3 5.2 %collective-permute-start.18 = (bf16[48,384]{1,0:T(8,128)(2,1)S(1)}, bf16[48,384]{1,0:T(8,128)(2,1)S(1)}, u32[]{:S(2)}, u32[]{:S(2)}) collective-permute-start(bf16[48,384]{1,0:T(8,128)(2,1)S(1)} %constant_dynamic-slice_fusion.5), channel_id=1, source_target_pairs={{0,16},{4,20},{8,24},{12,28},{16,0},{20,4},{24,8},{28,12},{1,17},{... | collective-permute-start | bytes 110600 | tf_op jit(solution)/shard_map/ppermute | solution.py:444
  97.6 4.9 %collective-permute-start.29 = (bf16[48,384]{1,0:T(8,128)(2,1)S(1)}, bf16[48,384]{1,0:T(8,128)(2,1)S(1)}, u32[]{:S(2)}, u32[]{:S(2)}) collective-permute-start(bf16[48,384]{1,0:T(8,128)(2,1)S(1)} %add_convert_fusion.13), channel_id=1, source_target_pairs={{0,16},{4,20},{8,24},{12,28},{16,0},{20,4},{24,8},{28,12},{1,17},{... | collective-permute-start | bytes 110600 | tf_op jit(solution)/shard_map/ppermute | solution.py:444
  99.6 5.3 %collective-permute-start.19 = (bf16[48,384]{1,0:T(8,128)(2,1)S(1)}, bf16[48,384]{1,0:T(8,128)(2,1)S(1)}, u32[]{:S(2)}, u32[]{:S(2)}) collective-permute-start(bf16[48,384]{1,0:T(8,128)(2,1)S(1)} %add_convert_fusion.14), channel_id=1, source_target_pairs={{0,16},{4,20},{8,24},{12,28},{16,0},{20,4},{24,8},{28,12},{1,17},{... | collective-permute-start | bytes 110600 | tf_op jit(solution)/shard_map/ppermute | solution.py:444
  102.5 4.4 %collective-permute-start.30 = (bf16[96,384]{1,0:T(8,128)(2,1)S(1)}, bf16[96,384]{1,0:T(8,128)(2,1)S(1)}, u32[]{:S(2)}, u32[]{:S(2)}) collective-permute-start(bf16[96,384]{1,0:T(8,128)(2,1)S(1)} %pad_maximum_fusion.14), channel_id=1, source_target_pairs={{0,4},{4,0},{8,12},{12,8},{16,20},{20,16},{24,28},{28,24},{1,5},{5... | collective-permute-start | bytes 221192 | tf_op jit(solution)/shard_map/ppermute | solution.py:444
  104.9 5.2 %collective-permute-start.20 = (bf16[96,384]{1,0:T(8,128)(2,1)S(1)}, bf16[96,384]{1,0:T(8,128)(2,1)S(1)}, u32[]{:S(2)}, u32[]{:S(2)}) collective-permute-start(bf16[96,384]{1,0:T(8,128)(2,1)S(1)} %pad_maximum_fusion.13), channel_id=1, source_target_pairs={{0,2},{2,0},{1,3},{3,1},{4,6},{6,4},{5,7},{7,5},{8,10},{10,8},{9,1... | collective-permute-start | bytes 221192 | tf_op jit(solution)/shard_map/ppermute | solution.py:444
  107.3 9.0 %collective-permute-start.5 = (bf16[512,384]{1,0:T(8,128)(2,1)S(1)}, bf16[512,384]{1,0:T(8,128)(2,1)S(1)}, u32[]{:S(2)}, u32[]{:S(2)}) collective-permute-start(bf16[512,384]{1,0:T(8,128)(2,1)S(1)} %constant_dynamic-slice_fusion.13), channel_id=1, source_target_pairs={{0,2},{2,0},{1,3},{3,1},{4,6},{6,4},{5,7},{7,5},{8,10},{10,8},{9,1... | collective-permute-start | bytes 1179656 | tf_op jit(solution)/shard_map/ppermute | solution.py:444
  108.2 14.2 %collective-permute-start.31 = (bf16[192,384]{1,0:T(8,128)(2,1)S(1)}, bf16[192,384]{1,0:T(8,128)(2,1)S(1)}, u32[]{:S(2)}, u32[]{:S(2)}) collective-permute-start(bf16[192,384]{1,0:T(8,128)(2,1)S(1)} %pad_maximum_fusion.11), channel_id=1, source_target_pairs={{0,2},{2,0},{1,3},{3,1},{4,6},{6,4},{5,7},{7,5},{8,10},{10,8},{9,1... | collective-permute-start | bytes 442376 | tf_op jit(solution)/shard_map/ppermute | solution.py:444
  110.2 6.7 %collective-permute-start.21 = (bf16[192,384]{1,0:T(8,128)(2,1)S(1)}, bf16[192,384]{1,0:T(8,128)(2,1)S(1)}, u32[]{:S(2)}, u32[]{:S(2)}) collective-permute-start(bf16[192,384]{1,0:T(8,128)(2,1)S(1)} %pad_maximum_fusion.10), channel_id=1, source_target_pairs={{0,8},{4,12},{8,0},{12,4},{16,24},{20,28},{24,16},{28,20},{1,9},{5... | collective-permute-start | bytes 442376 | tf_op jit(solution)/shard_map/ppermute | solution.py:444
  116.5 5.7 %collective-permute-start.6 = (bf16[256,384]{1,0:T(8,128)(2,1)S(1)}, bf16[256,384]{1,0:T(8,128)(2,1)S(1)}, u32[]{:S(2)}, u32[]{:S(2)}) collective-permute-start(bf16[256,384]{1,0:T(8,128)(2,1)S(1)} %constant_dynamic-slice_fusion.12), channel_id=1, source_target_pairs={{0,4},{4,0},{8,12},{12,8},{16,20},{20,16},{24,28},{28,24},{1,5},{5... | collective-permute-start | bytes 589832 | tf_op jit(solution)/shard_map/ppermute | solution.py:444
  117.0 17.4 %collective-permute-start.22 = (bf16[384,384]{1,0:T(8,128)(2,1)S(1)}, bf16[384,384]{1,0:T(8,128)(2,1)S(1)}, u32[]{:S(2)}, u32[]{:S(2)}) collective-permute-start(bf16[384,384]{1,0:T(8,128)(2,1)S(1)} %pad_maximum_fusion.7), channel_id=1, source_target_pairs={{0,4},{4,0},{8,12},{12,8},{16,20},{20,16},{24,28},{28,24},{1,5},{5... | collective-permute-start | bytes 884744 | tf_op jit(solution)/shard_map/ppermute | solution.py:444
  122.3 5.9 %collective-permute-start.7 = (bf16[128,384]{1,0:T(8,128)(2,1)S(1)}, bf16[128,384]{1,0:T(8,128)(2,1)S(1)}, u32[]{:S(2)}, u32[]{:S(2)}) collective-permute-start(bf16[128,384]{1,0:T(8,128)(2,1)S(1)} %constant_dynamic-slice_fusion.11), channel_id=1, source_target_pairs={{0,8},{4,12},{8,0},{12,4},{16,24},{20,28},{24,16},{28,20},{1,9},{5... | collective-permute-start | bytes 294920 | tf_op jit(solution)/shard_map/ppermute | solution.py:444
  128.2 5.3 %collective-permute-start.8 = (bf16[64,384]{1,0:T(8,128)(2,1)S(1)}, bf16[64,384]{1,0:T(8,128)(2,1)S(1)}, u32[]{:S(2)}, u32[]{:S(2)}) collective-permute-start(bf16[64,384]{1,0:T(8,128)(2,1)S(1)} %constant_dynamic-slice_fusion.10), channel_id=1, source_target_pairs={{0,16},{4,20},{8,24},{12,28},{16,0},{20,4},{24,8},{28,12},{1,17},{... | collective-permute-start | bytes 147464 | tf_op jit(solution)/shard_map/ppermute | solution.py:444
  129.3 14.6 %collective-permute-start.32 = (bf16[384,384]{1,0:T(8,128)(2,1)S(1)}, bf16[384,384]{1,0:T(8,128)(2,1)S(1)}, u32[]{:S(2)}, u32[]{:S(2)}) collective-permute-start(bf16[384,384]{1,0:T(8,128)(2,1)S(1)} %pad_maximum_fusion.8), channel_id=1, source_target_pairs={{0,8},{4,12},{8,0},{12,4},{16,24},{20,28},{24,16},{28,20},{1,9},{5... | collective-permute-start | bytes 884744 | tf_op jit(solution)/shard_map/ppermute | solution.py:444
  133.6 5.1 %collective-permute-start.9 = (bf16[64,384]{1,0:T(8,128)(2,1)S(1)}, bf16[64,384]{1,0:T(8,128)(2,1)S(1)}, u32[]{:S(2)}, u32[]{:S(2)}) collective-permute-start(bf16[64,384]{1,0:T(8,128)(2,1)S(1)} %add_convert_fusion.12), channel_id=1, source_target_pairs={{0,16},{4,20},{8,24},{12,28},{16,0},{20,4},{24,8},{28,12},{1,17},{... | collective-permute-start | bytes 147464 | tf_op jit(solution)/shard_map/ppermute | solution.py:444
  138.7 4.7 %collective-permute-start.10 = (bf16[128,384]{1,0:T(8,128)(2,1)S(1)}, bf16[128,384]{1,0:T(8,128)(2,1)S(1)}, u32[]{:S(2)}, u32[]{:S(2)}) collective-permute-start(bf16[128,384]{1,0:T(8,128)(2,1)S(1)} %pad_maximum_fusion.12), channel_id=1, source_target_pairs={{0,8},{4,12},{8,0},{12,4},{16,24},{20,28},{24,16},{28,20},{1,9},{5... | collective-permute-start | bytes 294920 | tf_op jit(solution)/shard_map/ppermute | solution.py:444
  138.8 11.3 %collective-permute-start.23 = (bf16[768,384]{1,0:T(8,128)(2,1)S(1)}, bf16[768,384]{1,0:T(8,128)(2,1)S(1)}, u32[]{:S(2)}, u32[]{:S(2)}) collective-permute-start(bf16[768,384]{1,0:T(8,128)(2,1)S(1)} %pad_maximum_fusion.3), channel_id=1, source_target_pairs={{0,1},{1,0},{2,3},{3,2},{4,5},{5,4},{6,7},{7,6},{8,9},{9,8},{10,11... | collective-permute-start | bytes 1769480 | tf_op jit(solution)/shard_map/ppermute | solution.py:444
  143.4 5.7 %collective-permute-start.11 = (bf16[256,384]{1,0:T(8,128)(2,1)S(1)}, bf16[256,384]{1,0:T(8,128)(2,1)S(1)}, u32[]{:S(2)}, u32[]{:S(2)}) collective-permute-start(bf16[256,384]{1,0:T(8,128)(2,1)S(1)} %pad_maximum_fusion.9), channel_id=1, source_target_pairs={{0,4},{4,0},{8,12},{12,8},{16,20},{20,16},{24,28},{28,24},{1,5},{5... | collective-permute-start | bytes 589832 | tf_op jit(solution)/shard_map/ppermute | solution.py:444
  144.1 13.3 %collective-permute-start.33 = (bf16[768,384]{1,0:T(8,128)(2,1)S(1)}, bf16[768,384]{1,0:T(8,128)(2,1)S(1)}, u32[]{:S(2)}, u32[]{:S(2)}) collective-permute-start(bf16[768,384]{1,0:T(8,128)(2,1)S(1)} %pad_maximum_fusion.4), channel_id=1, source_target_pairs={{0,1},{1,0},{2,3},{3,2},{4,5},{5,4},{6,7},{7,6},{8,9},{9,8},{10,11... | collective-permute-start | bytes 1769480 | tf_op jit(solution)/shard_map/ppermute | solution.py:444
  149.3 7.8 %collective-permute-start.12 = (bf16[512,384]{1,0:T(8,128)(2,1)S(1)}, bf16[512,384]{1,0:T(8,128)(2,1)S(1)}, u32[]{:S(2)}, u32[]{:S(2)}) collective-permute-start(bf16[512,384]{1,0:T(8,128)(2,1)S(1)} %pad_maximum_fusion.6), channel_id=1, source_target_pairs={{0,2},{2,0},{1,3},{3,1},{4,6},{6,4},{5,7},{7,5},{8,10},{10,8},{9,1... | collective-permute-start | bytes 1179656 | tf_op jit(solution)/shard_map/ppermute | solution.py:444
  157.4 3.6 %collective-permute-start.13 = (bf16[1024,384]{1,0:T(8,128)(2,1)S(1)}, bf16[1024,384]{1,0:T(8,128)(2,1)S(1)}, u32[]{:S(2)}, u32[]{:S(2)}) collective-permute-start(bf16[1024,384]{1,0:T(8,128)(2,1)S(1)} %pad_maximum_fusion.2), channel_id=1, source_target_pairs={{0,1},{1,0},{2,3},{3,2},{4,5},{5,4},{6,7},{7,6},{8,9},{9,8},{10,11... | collective-permute-start | bytes 2359304 | tf_op jit(solution)/shard_map/ppermute | solution.py:444
  162.1 2.4 %copy-start.1 = (bf16[1024,384]{1,0:T(8,128)(2,1)}, bf16[1024,384]{1,0:T(8,128)(2,1)S(1)}, u32[]{:S(2)}) copy-start(bf16[1024,384]{1,0:T(8,128)(2,1)S(1)} %get-tuple-element.70) | copy-start | bytes 2359300
  184.2 2.2 %copy-start.13 = (bf16[32,3072]{1,0:T(8,128)(2,1)}, bf16[32,3072]{1,0:T(8,128)(2,1)S(1)}, u32[]{:S(2)}) copy-start(bf16[32,3072]{1,0:T(8,128)(2,1)S(1)} %constant_dynamic-update-slice_fusion) | copy-start | bytes 589828
  191.3 3.9 %copy-start.2 = (bf16[1024,384]{1,0:T(8,128)(2,1)S(1)}, bf16[1024,384]{1,0:T(8,128)(2,1)}, u32[]{:S(2)}) copy-start(bf16[1024,384]{1,0:T(8,128)(2,1)} %copy-done.1) | copy-start | bytes 2359300
  191.3 3.9 %copy-start.3 = (bf16[1024,384]{1,0:T(8,128)(2,1)S(1)}, bf16[1024,384]{1,0:T(8,128)(2,1)}, u32[]{:S(2)}) copy-start(bf16[1024,384]{1,0:T(8,128)(2,1)} %get-tuple-element.69) | copy-start | bytes 2359300
  195.3 1.8 copy-start.4

commit v2 on v1

--- a/solution.py
+++ b/solution.py
@@ -20,9 +20,12 @@
 OUTC = 32
 BLOCKS = 4
 BLOCK = T // BLOCKS
-SMALL_AT = 1536
-SLOT_AT = 1600
-SLOT_ROWS = 48
+EARLY_SMALL = 1536
+EARLY_SLOTS = 1584
+EARLY_STEP = 32
+LATE_SMALL = 384
+LATE_SLOTS = 416
+LATE_STEP = 16
 
 exact_mode = lax.Precision.HIGHEST
 eps_norm = 1e-06
@@ -70,6 +73,10 @@
     )
 
 
+def row_of(ref):
+    return ref[...].reshape(1, ref.shape[0])
+
+
 def per_token(mods, index):
     rows = mods[:, index * W : (index + 1) * W]
     return jnp.concatenate(
@@ -110,17 +117,21 @@
 
 def front_kernel(
     meta,
-    patches_all,
+    patch_own,
+    patch_row,
+    patch_col,
+    patch_both,
     cot,
     mods_ref,
-    w_embed,
+    w_patch,
+    table,
     b_patch,
     b_query,
     b_value,
     b_proj,
     b_fc1,
     b_fc2,
-    w_out_t,
+    w_out,
     b_out,
     w_qkv_hbm,
     w_proj_hbm,
@@ -183,13 +194,16 @@
     level = lax.broadcasted_iota(jnp.int32, (32, ALL), 0)
     stacked = jnp.concatenate(
         [
-            patches_all[...],
+            jnp.concatenate(
+                [patch_own[...], patch_row[...], patch_col[...], patch_both[...]], axis=1
+            ),
             jnp.where(level == grid_row, 1.0, 0.0),
             jnp.where(level == grid_col, 1.0, 0.0),
         ],
         axis=0,
     )
-    hidden_all = mm(stacked.T, w_embed[...], exact_mode) + b_patch[...]
+    w_embed = jnp.concatenate([w_patch[...], table[...]], axis=0)
+    hidden_all = mm(stacked.T, w_embed, exact_mode) + row_of(b_patch)
     mods = mods_ref[...]
     shift_a = per_token(mods, 0)
     scale_a = 1.0 + per_token(mods, 1)
@@ -206,9 +220,9 @@
     copies[0].wait()
     w_qkv_low[...] = w_qkv_v[...].astype(low)
     entries = entry_all[...]
-    qkv_all[:, :W] = (mm(entries, w_qkv_low[:, :W]) + b_query[...]).astype(low)
+    qkv_all[:, :W] = (mm(entries, w_qkv_low[:, :W]) + row_of(b_query)).astype(low)
     qkv_all[:, W : 2 * W] = mm(entries, w_qkv_low[:, W : 2 * W]).astype(low)
-    qkv_all[:, 2 * W :] = (mm(entries, w_qkv_low[:, 2 * W :]) + b_value[...]).astype(low)
+    qkv_all[:, 2 * W :] = (mm(entries, w_qkv_low[:, 2 * W :]) + row_of(b_value)).astype(low)
     allowed = same_image(big, T, ALL)
     lane = lax.broadcasted_iota(jnp.int32, (T, 2 * HEAD_DIM), 1)
     stat = jnp.zeros((T, 2 * HEAD_DIM), full)
@@ -232,7 +246,7 @@
     attended_out[...] = attended
     copies[1].wait()
     w_proj_low = w_proj_v[...].astype(low)
-    attn_out = mm(attended, w_proj_low) + b_proj[...]
+    attn_out = mm(attended, w_proj_low) + row_of(b_proj)
     gate_a = per_token(mods, 2)
     hidden_mid = hidden_in + gate_a * attn_out
     normed_two, inv_two = norm_stats(hidden_mid)
@@ -241,52 +255,52 @@
     entry_two_out[...] = entry_two
     copies[2].wait()
     w_fc1_low = w_fc1_v[...].astype(low)
-    inner = mm(entry_two, w_fc1_low) + b_fc1[...]
+    inner = mm(entry_two, w_fc1_low) + row_of(b_fc1)
     activ, slope = gelu_parts(inner)
     inner_ref[...] = slope
     activ_low = activ.astype(low)
     activ_out[...] = activ_low
     copies[3].wait()
     w_fc2_low = w_fc2_v[...].astype(low)
-    mlp_out = mm(activ_low, w_fc2_low) + b_fc2[...]
+    mlp_out = mm(activ_low, w_fc2_low) + row_of(b_fc2)
     gate_m = per_token(mods, 5)
     hidden_out = hidden_mid + gate_m * mlp_out
     normed_three, inv_three = norm_stats(hidden_out)
     scale_f = 1.0 + per_token(mods, 7)
     entry_three = (normed_three * scale_f + per_token(mods, 6)).astype(low)
-    w_out_low = w_out_t[...].astype(low)
-    result[...] = mm_last(w_out_low, entry_three) + b_out[...]
+    w_out_low = w_out[...].T.astype(low)
+    out_bias = jnp.broadcast_to(row_of(b_out), (8, OUTC)).T[:, :1]
+    result[...] = mm_last(w_out_low, entry_three) + out_bias
     grad_out = cot[...].astype(low)
     small_out[...] = jnp.zeros_like(small_out)
-    small_out[PATCH : PATCH + OUTC] = mm(grad_out, entry_three)
-    at = PATCH + OUTC
+    small_out[:OUTC] = mm(grad_out, entry_three)
+    at = OUTC
     grad_out_tall = cot[...].T.astype(low)
     grad_b_out = jnp.sum(grad_out_tall.astype(full), axis=0, keepdims=True)
-    small_out[at + 9 : at + 10, :OUTC] = grad_b_out
+    small_out[at + 6 : at + 7, :OUTC] = grad_b_out
     grad_entry_three = mm(grad_out_tall, w_out_low)
-    slots_out[24:28] = block_sums(grad_entry_three)
-    slots_out[28:32] = block_sums(grad_entry_three * normed_three)
+    slots_out[16:20] = block_sums(grad_entry_three)
+    slots_out[20:24] = block_sums(grad_entry_three * normed_three)
     grad_hidden_out = norm_back(grad_entry_three * scale_f, normed_three, inv_three)
     grad_mlp = (gate_m * grad_hidden_out).astype(low)
     grad_mlp_out[...] = grad_mlp
-    slots_out[20:24] = block_sums(grad_hidden_out * mlp_out)
-    small_out[at + 8 : at + 9] = jnp.sum(grad_mlp.astype(full), axis=0, keepdims=True)
+    slots_out[12:16] = block_sums(grad_hidden_out * mlp_out)
+    small_out[at + 5 : at + 6] = jnp.sum(grad_mlp.astype(full), axis=0, keepdims=True)
     grad_activ = mm_last(grad_mlp, w_fc2_low)
     grad_inner = (grad_activ * inner_ref[...]).astype(low)
     grad_inner_out[...] = grad_inner
     grad_b_fc1 = jnp.sum(grad_inner.astype(full), axis=0, keepdims=True)
     for slab in range(FF // W):
-        small_out[at + 4 + slab : at + 5 + slab] = grad_b_fc1[:, slab * W : (slab + 1) * W]
+        small_out[at + 1 + slab : at + 2 + slab] = grad_b_fc1[:, slab * W : (slab + 1) * W]
     grad_entry_two = mm_last(grad_inner, w_fc1_low)
-    slots_out[12:16] = block_sums(grad_entry_two)
-    slots_out[16:20] = block_sums(grad_entry_two * normed_two)
+    slots_out[4:8] = block_sums(grad_entry_two)
+    slots_out[8:12] = block_sums(grad_entry_two * normed_two)
     grad_hidden_mid = grad_hidden_out + norm_back(grad_entry_two * scale_m, normed_two, inv_two)
     grad_mid_out[...] = grad_hidden_mid
     grad_attn = (gate_a * grad_hidden_mid).astype(low)
     grad_attn_out[...] = grad_attn
-    slots_out[0:8] = jnp.zeros((8, W), full)
-    slots_out[8:12] = block_sums(grad_hidden_mid * attn_out)
-    small_out[at + 3 : at + 4] = jnp.sum(grad_attn.astype(full), axis=0, keepdims=True)
+    slots_out[0:4] = block_sums(grad_hidden_mid * attn_out)
+    small_out[at : at + 1] = jnp.sum(grad_attn.astype(full), axis=0, keepdims=True)
     grad_attended = mm_last(grad_attn, w_proj_low).astype(low)
     payload[:, :W] = grad_attended
     for pair in range(HEADS // 2):
@@ -310,13 +324,7 @@
     qkv_all,
     payload,
     stat_ref,
-    activ,
-    grad_mlp,
-    entry_two,
-    grad_inner,
     grad_query_out,
-    grad_fc2,
-    grad_fc1,
 ):
     big = meta[0] == 1
     allowed = same_image(big, T, ALL)
@@ -339,27 +347,65 @@
         grad_query_out[:, cols] = (
             jnp.where(pair_half(T, 0), grads[0], grads[1]) * (1.0 / math.sqrt(HEAD_DIM))
         ).astype(low)
-    grad_fc2[...] = mm_rows(activ[...], grad_mlp[...]).astype(low)
+
+
+def slot_rows(meta, sums, act_ref, count, step):
+    big = meta[0] == 1
+    slot_line = lax.broadcasted_iota(jnp.int32, (BLOCKS, W), 0)
+    joined = []
+    for block in range(count):
+        part = sums[4 * block : 4 * block + 4]
+        whole = jnp.where(slot_line == 0, jnp.sum(part, axis=0, keepdims=True), 0.0)
+        joined.append(jnp.where(big, whole, part))
+    first_tile = (meta[1] == 0) & (meta[2] == 0)
+    joined.append(jnp.where(first_tile, act_ref[...], 0.0))
+    joined.append(jnp.zeros((step - 4 * count - 4, W), full))
+    return jnp.concatenate(joined, axis=0).astype(low)
+
+
+def early_kernel(
+    meta,
+    activ,
+    grad_mlp,
+    entry_two,
+    grad_inner,
+    attended,
+    grad_attn,
+    small,
+    slots,
+    act_ref,
+    bundle,
+):
+    half = bundle.shape[1]
+    first = bundle.at[meta[2]]
+    second = bundle.at[1 - meta[2]]
+    first[:FF] = mm_rows(activ[...], grad_mlp[...]).astype(low)
+    first[FF : FF + W] = mm_rows(attended[...], grad_attn[...]).astype(low)
+    if half > FF + W:
+        first[FF + W :] = jnp.zeros((half - FF - W, W), low)
     entry = entry_two[...]
     for slab in range(FF // W):
-        grad_fc1[slab * W : (slab + 1) * W] = mm_rows(
+        second[slab * W : (slab + 1) * W] = mm_rows(
             entry, grad_inner[:, slab * W : (slab + 1) * W]
         ).astype(low)
+    second[EARLY_SMALL:EARLY_SLOTS] = small[...].astype(low)
+    second[EARLY_SLOTS:] = jnp.zeros((half - EARLY_SLOTS, W), low)
+    start = pl.multiple_of(EARLY_SLOTS + meta[3] * EARLY_STEP, 16)
+    second[pl.ds(start, EARLY_STEP)] = slot_rows(meta, slots[...], act_ref, 6, EARLY_STEP)
 
 
 def key_kernel(
     meta,
     qkv_all,
-    payload_all,
+    pay_own,
+    pay_row,
+    pay_col,
+    pay_both,
     grad_query,
     entry_own,
     normed_own,
     inv_own,
-    attended,
-    grad_attn,
     grad_mid,
-    small,
-    slots,
     mods_ref,
     act_ref,
     patches,
@@ -372,7 +418,8 @@
 ):
     big = meta[0] == 1
     allowed = same_image(big, T, ALL)
-    packed = payload_all[:, W:].astype(full)
+    tiles = (pay_own, pay_row, pay_col, pay_both)
+    packed = jnp.concatenate([tile[:, W:] for tile in tiles], axis=0).astype(full)
     stat = packed + pltpu.roll(packed, 112, 1) + pltpu.roll(packed, 96, 1)
     stat_t = stat.T
     for pair in range(HEADS // 2):
@@ -380,7 +427,7 @@
         q_pair = qkv_all[:, cols]
         k_pair = qkv_all[:T, W + cols.start : W + cols.stop] * low(1.0 / math.sqrt(HEAD_DIM))
         v_pair = qkv_all[:T, 2 * W + cols.start : 2 * W + cols.stop]
-        do_pair = payload_all[:, cols]
+        do_pair = jnp.concatenate([tile[:, cols] for tile in tiles], axis=0)
         grad_k = []
         grad_v = []
         for half in range(2):
@@ -401,10 +448,14 @@
     grad_q = grad_query[...]
     grad_k = gk_ref[...]
     grad_v = gv_ref[...]
-    bundle[:W] = mm_rows(entry, grad_q).astype(low)
-    bundle[W : 2 * W] = mm_rows(entry, grad_k).astype(low)
-    bundle[2 * W : 3 * W] = mm_rows(entry, grad_v).astype(low)
-    bundle[3 * W : 4 * W] = mm_rows(attended[...], grad_attn[...]).astype(low)
+    half = bundle.shape[1]
+    first = bundle.at[meta[2]]
+    second = bundle.at[1 - meta[2]]
+    first[:W] = mm_rows(entry, grad_q).astype(low)
+    first[W : 2 * W] = mm_rows(entry, grad_k).astype(low)
+    if half > 2 * W:
+        first[2 * W :] = jnp.zeros((half - 2 * W, W), low)
+    second[:W] = mm_rows(entry, grad_v).astype(low)
     grad_entry = (
         mm_last(grad_q, w_qkv_low[:, :W])
         + mm_last(grad_k, w_qkv_low[:, W : 2 * W])
@@ -414,29 +465,161 @@
     scale_a = 1.0 + per_token(mods_ref[...], 1)
     grad_in = grad_mid[...] + norm_back(grad_entry * scale_a, normed, inv_own[...])
     grad_patches[...] = mm_last(w_patch[...], grad_in, exact_mode)
-    at = PATCH + OUTC
-    line = lax.broadcasted_iota(jnp.int32, small.shape, 0)
-    tail = small[...]
-    tail = jnp.where(line == at, jnp.sum(grad_in, axis=0, keepdims=True), tail)
-    tail = jnp.where(line == at + 1, jnp.sum(grad_q.astype(full), axis=0, keepdims=True), tail)
-    tail = jnp.where(line == at + 2, jnp.sum(grad_v.astype(full), axis=0, keepdims=True), tail)
-    grad_w_patch = mm(patches[...], grad_in, exact_mode)
-    tail = jnp.concatenate([grad_w_patch, tail[PATCH:]], axis=0)
-    bundle[SMALL_AT:SLOT_AT] = tail.astype(low)
-    bundle[SLOT_AT:] = jnp.zeros((bundle.shape[0] - SLOT_AT, W), low)
-    late = jnp.concatenate([block_sums(grad_entry), block_sums(grad_entry * normed)], axis=0)
-    sums = jnp.concatenate([late, slots[8:]], axis=0)
-    joined = []
-    slot_line = lax.broadcasted_iota(jnp.int32, (BLOCKS, W), 0)
-    for block in range(8):
-        part = sums[4 * block : 4 * block + 4]
-        whole = jnp.where(slot_line == 0, jnp.sum(part, axis=0, keepdims=True), 0.0)
-        joined.append(jnp.where(big, whole, part))
-    first_tile = (meta[1] == 0) & (meta[2] == 0)
-    joined.append(jnp.where(first_tile, act_ref[...], 0.0))
-    joined.append(jnp.zeros((SLOT_ROWS - 36, W), full))
-    start = pl.multiple_of(SLOT_AT + meta[3] * SLOT_ROWS, 16)
-    bundle[pl.ds(start, SLOT_ROWS)] = jnp.concatenate(joined, axis=0).astype(low)
+    second[LATE_SMALL:LATE_SLOTS] = jnp.concatenate(
+        [
+            mm(patches[...], grad_in, exact_mode),
+            jnp.sum(grad_in, axis=0, keepdims=True),
+            jnp.sum(grad_q.astype(full), axis=0, keepdims=True),
+            jnp.sum(grad_v.astype(full), axis=0, keepdims=True),
+            jnp.zeros((LATE_SLOTS - LATE_SMALL - PATCH - 3, W), full),
+        ],
+        axis=0,
+    ).astype(low)
+    second[LATE_SLOTS:] = jnp.zeros((half - LATE_SLOTS, W), low)
+    sums = jnp.concatenate([block_sums(grad_entry), block_sums(grad_entry * normed)], axis=0)
+    start = pl.multiple_of(LATE_SLOTS + meta[3] * LATE_STEP, 16)
+    second[pl.ds(start, LATE_STEP)] = slot_rows(meta, sums, act_ref, 2, LATE_STEP)
+
+
+def slot_products(region, count, step):
+    rows = region.shape[0]
+    place = lax.broadcasted_iota(jnp.int32, (rows, W), 0) & (step - 1)
+    region_full = region.astype(full)
+    acts = jnp.where(place >> 2 == count, region_full, 0.0)
+    products = []
+    sums = []
+    for block in range(count):
+        turned = pltpu.roll(acts, rows - 4 * (count - block), 0).astype(low)
+        products.append(mm_rows(turned, region))
+        sums.append(
+            jnp.sum(jnp.where(place >> 2 == block, region_full, 0.0), axis=0, keepdims=True)
+        )
+    return products, sums
+
+
+def slot_back(rows, weight_ref, at, block):
+    weight = weight_ref[:, at * W : (at + 1) * W]
+    high = weight.astype(low)
+    rest = (weight - high.astype(full)).astype(low)
+    return (mm_last(rows, high) + mm_last(rows, rest))[4 * block : 4 * block + 4]
+
+
+def unpack_early_kernel(
+    groups,
+    meta,
+    own,
+    other,
+    w_mod,
+    w_fmod,
+    g_fc2,
+    g_proj,
+    g_fc1,
+    g_w_out,
+    g_b_proj,
+    g_b_fc1,
+    g_b_fc2,
+    g_b_out,
+    g_w_mod,
+    g_w_fmod,
+    b_mod_part,
+    g_b_fmod,
+    act_part,
+    work,
+    sem,
+):
+    even = meta[2] == 0
+
+    def first(lo, hi):
+        return jnp.where(even, own[lo:hi], other[lo:hi])
+
+    def second(lo, hi):
+        return jnp.where(even, other[lo:hi], own[lo:hi])
+
+    region = second(EARLY_SLOTS, EARLY_SLOTS + EARLY_STEP * groups)
+    products, sums = slot_products(region, 6, EARLY_STEP)
+    for block in range(4):
+        work[:, block * W : (block + 1) * W] = products[block]
+    copy = pltpu.make_async_copy(work, g_w_mod.at[:, 2 * W : 6 * W], sem)
+    copy.start()
+    for block in range(2):
+        g_w_fmod[:, block * W : (block + 1) * W] = products[4 + block]
+    b_mod_part[...] = jnp.concatenate(sums[:4], axis=1)[0]
+    g_b_fmod[...] = jnp.concatenate(sums[4:], axis=1)[0]
+    start = pl.multiple_of(EARLY_SLOTS + meta[3] * EARLY_STEP, 16)
+    rows = jnp.where(even, other[pl.ds(start, EARLY_STEP)], own[pl.ds(start, EARLY_STEP)])
+    total = slot_back(rows, w_mod, 2, 0)
+    for block in range(1, 4):
+        total = total + slot_back(rows, w_mod, 2 + block, block)
+    for block in range(2):
+        total = total + slot_back(rows, w_fmod, block, 4 + block)
+    act_part[...] = total
+    g_fc2[...] = first(0, FF).astype(full)
+    g_proj[...] = first(FF, FF + W).astype(full)
+    for slab in range(FF // W):
+        g_fc1[:, slab * W : (slab + 1) * W] = second(slab * W, (slab + 1) * W).astype(full)
+    small = second(EARLY_SMALL, EARLY_SLOTS).astype(full)
+    g_w_out[...] = small[:OUTC].T
+    at = OUTC
+    g_b_proj[...] = small[at : at + 1][0]
+    g_b_fc1[...] = jnp.concatenate([small[at + 1 + i : at + 2 + i] for i in range(4)], axis=1)[0]
+    g_b_fc2[...] = small[at + 5 : at + 6][0]
+    g_b_out[...] = small[at + 6 : at + 7, :OUTC][0]
+    copy.wait()
+
+
+def unpack_late_kernel(
+    groups,
+    meta,
+    own,
+    other,
+    cond,
+    act_part,
+    b_mod_part,
+    w_mod_front,
+    w_mod_in,
+    g_w_mod,
+    g_cond,
+    g_w_patch,
+    g_b_patch,
+    g_b_mod,
+    g_w_qkv,
+    g_b_query,
+    g_b_value,
+    work,
+    sem,
+):
+    even = meta[2] == 0
+
+    def first(lo, hi):
+        return jnp.where(even, own[lo:hi], other[lo:hi])
+
+    def second(lo, hi):
+        return jnp.where(even, other[lo:hi], own[lo:hi])
+
+    region = second(LATE_SLOTS, LATE_SLOTS + LATE_STEP * groups)
+    products, sums = slot_products(region, 2, LATE_STEP)
+    for block in range(2):
+        work[:, block * W : (block + 1) * W] = products[block]
+    copy = pltpu.make_async_copy(work, g_w_mod.at[:, : 2 * W], sem)
+    copy.start()
+    g_b_mod[...] = jnp.concatenate(sums + [row_of(b_mod_part)], axis=1)[0]
+    start = pl.multiple_of(LATE_SLOTS + meta[3] * LATE_STEP, 16)
+    rows = jnp.where(even, other[pl.ds(start, LATE_STEP)], own[pl.ds(start, LATE_STEP)])
+    total = act_part[...]
+    for block in range(2):
+        total = total + slot_back(rows, w_mod_front, block, block)
+    value = cond[...]
+    gate = 1.0 / (1.0 + jnp.exp(-value))
+    g_cond[...] = total * gate * (1.0 + value * (1.0 - gate))
+    for slab in range(2):
+        g_w_qkv[:, slab * W : (slab + 1) * W] = first(slab * W, (slab + 1) * W).astype(full)
+    g_w_qkv[:, 2 * W :] = second(0, W).astype(full)
+    small = second(LATE_SMALL, LATE_SLOTS).astype(full)
+    g_w_patch[...] = small[:PATCH]
+    g_b_patch[...] = small[PATCH : PATCH + 1][0]
+    g_b_query[...] = small[PATCH + 1 : PATCH + 2][0]
+    g_b_value[...] = small[PATCH + 2 : PATCH + 3][0]
+    copy.wait()
 
 
 def bit_swap(array, axis_name, bit):
@@ -446,13 +629,6 @@
 
 def bit_here(axis_name, bit):
     return (lax.axis_index(axis_name) >> bit) & 1
-
-
-def join_halves(mine, other, axis_name, bit):
-    low_side = bit_here(axis_name, bit) == 0
-    return jnp.concatenate(
-        [jnp.where(low_side, mine, other), jnp.where(low_side, other, mine)], axis=0
-    )
 
 
 def batch_bits():
@@ -461,37 +637,61 @@
     return size.bit_length() - 1
 
 
-def halve_step(part, axis_name, bit):
-    half = part.shape[0] // 2
-    here = bit_here(axis_name, bit)
-    keep = lax.dynamic_slice_in_dim(part, here * half, half, 0)
-    send = lax.dynamic_slice_in_dim(part, (1 - here) * half, half, 0)
-    got = bit_swap(send, axis_name, bit)
-    return (keep.astype(jnp.float32) + got.astype(jnp.float32)).astype(jnp.bfloat16)
-
-
-def colour_orders():
+def two_way_swap(array, pair):
+    sizes = [lax.axis_size(name) for name in ("batch", "row", "col")]
+    moves = []
+    for group in range(sizes[0]):
+        for row in range(sizes[1]):
+            for col in range(sizes[2]):
+                place = {"batch": group, "row": row}
+                axis_name, bit = pair[col]
+                place[axis_name] ^= 1 << bit
+                moves.append(
+                    (
+                        (group * sizes[1] + row) * sizes[2] + col,
+                        (place["batch"] * sizes[1] + place["row"]) * sizes[2] + col,
+                    )
+                )
+    return lax.ppermute(array, ("batch", "row", "col"), moves)
+
+
+def sum_halves(stack, orders):
+    core = lax.axis_index("col")
+    got = bit_swap(stack[1], "col", 0)
+    part = (stack[0].astype(full) + got.astype(full)).astype(low)
+    pairs = list(zip(*orders))
+    heres = [jnp.where(core == 0, bit_here(*pair[0]), bit_here(*pair[1])) for pair in pairs]
+    for pair, here in zip(pairs, heres):
+        half = part.shape[0] // 2
+        keep = lax.dynamic_slice_in_dim(part, here * half, half, 0)
+        send = lax.dynamic_slice_in_dim(part, (1 - here) * half, half, 0)
+        got = two_way_swap(send, pair)
+        part = (keep.astype(full) + got.astype(full)).astype(low)
+    for pair, here in zip(reversed(pairs), reversed(heres)):
+        got = two_way_swap(part, pair)
+        part = jnp.concatenate(
+            [jnp.where(here == 0, part, got), jnp.where(here == 0, got, part)], axis=0
+        )
+    return part, bit_swap(part, "col", 0)
+
+
+def link_orders():
     bits = [("batch", bit) for bit in range(batch_bits())]
-    first = ("col", 0)
-    second = ("row", 0)
-    return (
-        [first, second] + bits,
-        [first] + bits[:2] + [second] + bits[2:],
-        [first] + bits[1:2] + [second] + bits[:1] + bits[2:],
-    )
-
-
-def sum_rows(parts):
-    orders = colour_orders()
-    depth = len(orders[0])
-    for step in range(depth):
-        parts = [halve_step(part, *order[step]) for part, order in zip(parts, orders)]
-    for step in reversed(range(depth)):
-        parts = [
-            join_halves(part, bit_swap(part, *order[step]), *order[step])
-            for part, order in zip(parts, orders)
-        ]
-    return parts
+    row = [("row", 0)]
+    early = (bits[:1] + row + bits[1:], bits[1:2] + bits[:1] + row + bits[2:])
+    late = (row + bits, bits[:2] + row + bits[2:])
+    return early, late
+
+
+def cost(microseconds):
+    return pl.CostEstimate(
+        flops=int(microseconds * 1e9), bytes_accessed=0, transcendentals=0
+    )
+
+
+def half_rows(needed, devices):
+    unit = 8 * devices // 2
+    return -(-needed // unit) * unit
 
 
 def shaped(*pairs):
@@ -501,24 +701,22 @@
 vmem = pl.BlockSpec(memory_space=pltpu.VMEM)
 smem = pl.BlockSpec(memory_space=pltpu.SMEM)
 hbm = pl.BlockSpec(memory_space=pl.ANY)
-
-
-def unslab(stacked, first, count):
-    return jnp.concatenate(
-        [stacked[(first + at) * W : (first + at + 1) * W] for at in range(count)], axis=1
-    ).astype(full)
 
 
 def position_table():
     quarter = W // 4
     rates = 1.0 / jnp.power(10000.0, jnp.arange(quarter, dtype=full) / quarter)
     angle = jnp.arange(32, dtype=full)[:, None] * rates[None, :]
-    return jnp.concatenate([jnp.sin(angle), jnp.cos(angle)], axis=1)
-
-
-def gather_tiles(array, axis):
-    array = jnp.concatenate([array, bit_swap(array, "row", 0)], axis=axis)
-    return jnp.concatenate([array, bit_swap(array, "col", 0)], axis=axis)
+    waves = jnp.concatenate([jnp.sin(angle), jnp.cos(angle)], axis=1)
+    return jnp.concatenate(
+        [jnp.pad(waves, ((0, 0), (0, W // 2))), jnp.pad(waves, ((0, 0), (W // 2, 0)))], axis=0
+    )
+
+
+def tile_copies(array):
+    by_row = bit_swap(array, "row", 0)
+    by_col = bit_swap(array, "col", 0)
+    return array, by_row, by_col, bit_swap(by_row, "col", 0)
 
 
 def body(
@@ -546,9 +744,8 @@
 ):
     groups = lax.axis_size("batch")
     devices = groups * lax.axis_size("row") * lax.axis_size("col")
-    slot_count = image_lengths.shape[2]
     patch_cols = patches[0, 0, 0]
-    patches_all = gather_tiles(patch_cols, 1)
+    patch_tiles = tile_copies(patch_cols)
     big = image_lengths[0, 0, 0] == BIG_LEN
     group = lax.axis_index("batch")
     meta = jnp.stack(
@@ -563,16 +760,6 @@
         axis=1,
     )
     mods = jnp.where(big, mods[:1], mods)
-    table = position_table()
-    blank = jnp.zeros_like(table)
-    w_embed = jnp.concatenate(
-        [
-            w_patch,
-            jnp.concatenate([table, blank], axis=1),
-            jnp.concatenate([blank, table], axis=1),
-        ],
-        axis=0,
-    )
     (
         result,
         payload,
@@ -593,10 +780,11 @@
         stat,
     ) = pl.pallas_call(
         lambda *refs: front_kernel(
-            *refs[:33], *refs[34:40], refs[33], *refs[40:]
+            *refs[:37], *refs[38:44], refs[37], *refs[44:]
         ),
         name="front",
-        in_specs=[smem] + [vmem] * 12 + [hbm] * 4,
+        in_specs=[smem] + [vmem] * 16 + [hbm] * 4,
+        cost_estimate=cost(16),
         out_specs=[vmem] * 17,
         out_shape=shaped(
             ((OUTC, T), full),
@@ -612,8 +800,8 @@
             ((T, W), low),
             ((T, W), low),
             ((T, FF), low),
-            ((64, W), full),
-            ((32, W), full),
+            ((48, W), full),
+            ((24, W), full),
             ((W, 3 * W), low),
             ((T, 128), full),
         ),
@@ -629,102 +817,173 @@
         ],
     )(
         meta,
-        patches_all,
+        *patch_tiles,
         cotangent[0, 0, 0],
         mods,
-        w_embed,
-        b_patch[None],
-        b_query[None],
-        b_value[None],
-        b_proj[None],
-        b_fc1[None],
-        b_fc2[None],
-        w_out.T,
-        b_out[:, None],
+        w_patch,
+        position_table(),
+        b_patch,
+        b_query,
+        b_value,
+        b_proj,
+        b_fc1,
+        b_fc2,
+        w_out,
+        b_out,
         w_qkv,
         w_proj,
         w_fc1,
         w_fc2,
     )
-    payload_all = gather_tiles(payload, 0)
-    grad_query, grad_fc2, grad_fc1 = pl.pallas_call(
+    payload_tiles = tile_copies(payload)
+    early_half = half_rows(max(FF + W, EARLY_SLOTS + groups * EARLY_STEP), devices)
+    early = pl.pallas_call(
+        early_kernel,
+        name="early_side",
+        in_specs=[smem] + [vmem] * 9,
+        out_specs=vmem,
+        out_shape=jax.ShapeDtypeStruct((2, early_half, W), low),
+        cost_estimate=cost(3),
+    )(
+        meta,
+        activ,
+        grad_mlp,
+        entry_two,
+        grad_inner,
+        attended,
+        grad_attn,
+        small,
+        slots,
+        act,
+    )
+    early_orders, late_orders = link_orders()
+    early_own, early_other = sum_halves(early, early_orders)
+    grad_query = pl.pallas_call(
         query_kernel,
         name="query_side",
-        in_specs=[smem] + [vmem] * 7,
-        out_specs=[vmem] * 3,
-        out_shape=shaped(((T, W), low), ((FF, W), low), ((FF, W), low)),
-    )(meta, qkv_all, payload, stat, activ, grad_mlp, entry_two, grad_inner)
-    unit = 16 * devices
-    rows = -(-(SLOT_AT + groups * SLOT_ROWS) // unit) * unit
-    bundle, grad_patch_cols = pl.pallas_call(
+        in_specs=[smem] + [vmem] * 3,
+        out_specs=vmem,
+        out_shape=jax.ShapeDtypeStruct((T, W), low),
+        cost_estimate=cost(5),
+    )(meta, qkv_all, payload, stat)
+    late_half = half_rows(max(2 * W, LATE_SLOTS + groups * LATE_STEP), devices)
+    late, grad_patch_cols = pl.pallas_call(
         key_kernel,
         name="key_side",
-        in_specs=[smem] + [vmem] * 16,
+        in_specs=[smem] + [vmem] * 15,
         out_specs=[vmem] * 2,
-        out_shape=shaped(((rows, W), low), ((PATCH, T), full)),
+        out_shape=shaped(((2, late_half, W), low), ((PATCH, T), full)),
         scratch_shapes=[pltpu.VMEM((T, W), low), pltpu.VMEM((T, W), low)],
+        cost_estimate=cost(9),
     )(
         meta,
         qkv_all,
-        payload_all,
+        *payload_tiles,
         grad_query,
         entry_own,
         normed_own,
         inv_own,
-        attended,
-        grad_attn,
         grad_mid,
-        small,
-        slots,
         mods,
         act,
         patch_cols,
         w_patch,
         w_qkv_low,
     )
-    late, fc1_sum, fc2_sum = sum_rows([bundle, grad_fc1, grad_fc2])
-    tail = late[SMALL_AT:SLOT_AT].astype(full)
-    by_group = late[SLOT_AT : SLOT_AT + groups * SLOT_ROWS].reshape(groups, SLOT_ROWS, W)
-    grad_slots_all = jnp.concatenate(
-        [
-            by_group[:, 4 * block : 4 * block + 4].reshape(groups * slot_count, W)
-            for block in range(8)
-        ],
-        axis=1,
-    )
-    act_all = by_group[:, 32:36].reshape(groups * slot_count, W)
-    grad_w_mods = lax.dot_general(
-        act_all, grad_slots_all, (((0,), (0,)), ((), ())), preferred_element_type=full
-    )
-    grad_b_mods = jnp.sum(grad_slots_all.astype(full), axis=0)
-    grad_slots = lax.dynamic_slice_in_dim(grad_slots_all, group * slot_count, slot_count, 0).astype(
-        full
-    )
-    grad_act = lax.dot_general(
-        grad_slots[:, : 6 * W], w_mod, (((1,), (1,)), ((), ())), precision=exact_mode
-    ) + lax.dot_general(
-        grad_slots[:, 6 * W :], w_fmod, (((1,), (1,)), ((), ())), precision=exact_mode
-    )
-    grad_cond = jax.vjp(jax.nn.silu, cond[0])[1](grad_act)[0][None]
-    at = PATCH + OUTC
+    late_own, late_other = sum_halves(late, late_orders)
+    (
+        g_fc2,
+        g_proj,
+        g_fc1,
+        g_w_out,
+        g_b_proj,
+        g_b_fc1,
+        g_b_fc2,
+        g_b_out,
+        g_w_mod,
+        g_w_fmod,
+        b_mod_part,
+        g_b_fmod,
+        act_part,
+    ) = pl.pallas_call(
+        lambda *refs: unpack_early_kernel(groups, *refs),
+        name="unpack_early",
+        in_specs=[smem] + [vmem] * 4,
+        out_specs=[vmem] * 8 + [hbm] + [vmem] * 4,
+        out_shape=shaped(
+            ((FF, W), full),
+            ((W, W), full),
+            ((W, FF), full),
+            ((W, OUTC), full),
+            ((W,), full),
+            ((FF,), full),
+            ((W,), full),
+            ((OUTC,), full),
+            ((W, 6 * W), full),
+            ((W, 2 * W), full),
+            ((4 * W,), full),
+            ((2 * W,), full),
+            ((4, W), full),
+        ),
+        scratch_shapes=[pltpu.VMEM((W, 4 * W), full), pltpu.SemaphoreType.DMA(())],
+        cost_estimate=cost(8),
+    )(meta, early_own, early_other, w_mod, w_fmod)
+    (
+        g_w_mod,
+        g_cond,
+        g_w_patch,
+        g_b_patch,
+        g_b_mod,
+        g_w_qkv,
+        g_b_query,
+        g_b_value,
+    ) = pl.pallas_call(
+        lambda *refs: unpack_late_kernel(groups, *refs),
+        name="unpack_late",
+        in_specs=[smem] + [vmem] * 6 + [hbm],
+        out_specs=[hbm] + [vmem] * 7,
+        out_shape=shaped(
+            ((W, 6 * W), full),
+            ((4, W), full),
+            ((PATCH, W), full),
+            ((W,), full),
+            ((6 * W,), full),
+            ((W, 3 * W), full),
+            ((W,), full),
+            ((W,), full),
+        ),
+        scratch_shapes=[pltpu.VMEM((W, 2 * W), full), pltpu.SemaphoreType.DMA(())],
+        input_output_aliases={7: 0},
+        cost_estimate=cost(5),
+    )(
+        meta,
+        late_own,
+        late_other,
+        cond[0],
+        act_part,
+        b_mod_part,
+        w_mod[:, : 2 * W],
+        g_w_mod,
+    )
+    grad_cond = g_cond[None]
     summed = (
-        tail[:PATCH],
-        tail[at],
-        grad_w_mods[:, : 6 * W],
-        grad_b_mods[: 6 * W],
-        unslab(late, 0, 3),
-        tail[at + 1],
-        tail[at + 2],
-        unslab(late, 3, 1),
-        tail[at + 3],
-        unslab(fc1_sum, 0, FF // W),
-        tail[at + 4 : at + 8].reshape(FF),
-        fc2_sum.astype(full),
-        tail[at + 8],
-        grad_w_mods[:, 6 * W :],
-        grad_b_mods[6 * W :],
-        tail[PATCH:at].T,
-        tail[at + 9, :OUTC],
+        g_w_patch,
+        g_b_patch,
+        g_w_mod,
+        g_b_mod,
+        g_w_qkv,
+        g_b_query,
+        g_b_value,
+        g_proj,
+        g_b_proj,
+        g_fc1,
+        g_b_fc1,
+        g_fc2,
+        g_b_fc2,
+        g_w_fmod,
+        g_b_fmod,
+        g_w_out,
+        g_b_out,
     )
     return (result[None, None, None], grad_patch_cols[None, None, None], grad_cond) + tuple(
         summed

time: 201 us -> 151 us (0.75)
  local copies, waits for them, and re-layouts: 43.7 us -> 10 us
  waiting for transfers between devices: 58.6 us -> 38.5 us
  Pallas kernels: 33.5 us -> 49 us
  other arithmetic: 22.6 us -> 9.81 us
  starting transfers between devices: 28.3 us -> 34.1 us
  matrix products: 10.4 us -> 5.66 us
    ppermute x34 -> x10, waiting for transfers between devices: 58.6 us -> 2.66 us  [bit_swap(): lax.ppermute(array, axis_name, [(i, i ^ 1 << bit) for i in range(size)])]
    ppermute x0 -> x16, waiting for transfers between devices: none -> 35.9 us  [two_way_swap(): return lax.ppermute(array, ('batch', 'row', 'col'), moves)]
    ppermute x0 -> x16, starting transfers between devices: none -> 28.8 us  [two_way_swap(): return lax.ppermute(array, ('batch', 'row', 'col'), moves)]
    ppermute x34 -> x10, starting transfers between devices: 28.3 us -> 5.29 us  [bit_swap(): lax.ppermute(array, axis_name, [(i, i ^ 1 << bit) for i in range(size)])]
    pallas_call x2 -> x5, Pallas kernels: 26.1 us -> 43.3 us  [the longest x1 16.4 us: body(): pl.pallas_call(lambda *refs: front_kernel(*refs[:37], *refs[38:44], refs[...]
    reshape x10 -> x0, local copies, waits for them, and re-layouts: 12.7 us -> none  [the longest x8 10.8 us: body(): by_group[:, 4 * block:4 * block + 4].reshape(groups * slot_count, W)]
    broadcast_in_dim x8 -> x0, local copies, waits for them, and re-layouts: 8.86 us -> none  [the longest x1 1.34 us: body(): b_out[:, None]]
    dot_general x3 -> x0, matrix products: 6.06 us -> none  [the longest x1 2.59 us: body(): lax.dot_general(grad_slots[:, :6 * W], w_mod, (((1,), (1,)), ((), ())), p...]
  transfers between devices with their start and end apart: 34 -> 26, of which waited for: 18 -> 14; matrix products, arithmetic and copies ran while one was open for 17% -> 13% of each run, Pallas kernels for 5% -> 16%
where the time goes in v2:
time: 151 us; the launch traced here: 149 us
  Pallas kernels  49 us (32%)
  waiting for transfers between devices  38.5 us (25%)
  starting transfers between devices  34.1 us (23%)
  local copies, waits for them, and re-layouts  10 us (7%)
  other arithmetic  9.81 us (6%)
  matrix products  5.66 us (4%)
  between operations  1.83 us (1%)
    ppermute x16, waiting for transfers between devices, two_way_swap(): return lax.ppermute(array, ('batch', 'row', 'col'), moves)  35.9 us
    ppermute x16, starting transfers between devices, two_way_swap(): return lax.ppermute(array, ('batch', 'row', 'col'), moves)  28.8 us
    pallas_call x1, Pallas kernels, body(): pl.pallas_call(lambda *refs: front_kernel(*refs[:37], *refs[38:44], refs[...  16.4 us
    pallas_call x1, Pallas kernels, body(): pl.pallas_call(key_kernel, name='key_side', in_specs=[smem] + [vmem] * 15...  9.32 us
    pallas_call x1, Pallas kernels, body(): pl.pallas_call(lambda *refs: unpack_early_kernel(groups, *refs), name='un...  8.89 us
    pallas_call x1, Pallas kernels, body(): pl.pallas_call(query_kernel, name='query_side', in_specs=[smem] + [vmem]...  5.66 us
    ppermute x10, starting transfers between devices, bit_swap(): lax.ppermute(array, axis_name, [(i, i ^ 1 << bit) for i in range(size)])  5.29 us
    unnamed x26, local copies, waits for them, and re-layouts  5.07 us
  transfers between devices with their start and end apart: 26, of which 14 were waited for; matrix products, arithmetic and copies ran while one was open for 13% of the time, Pallas kernels for 16%

profile of v2, /device:TPU:0, one launch (start us, length us, event | category | flops | bytes accessed | tf_op | source)
XLA Modules:
  0.0 148.9 jit_solution(5499964240162565801)
XLA Ops:
  0.7 0.6 collective-permute-start.1
  1.2 2.6 %collective-permute-start = (f32[16,256]{1,0:T(8,128)}, f32[16,256]{1,0:T(8,128)S(1)}, u32[]{:S(2)}, u32[]{:S(2)}) collective-permute-start(f32[16,256]{1,0:T(8,128)} %bitcast.34), channel_id=1, source_target_pairs={{0,2},{2,0},{1,3},{3,1},{4,6},{6,4},{5,7},{7,5},{8,10},{10,8},{9,1... | collective-permute-start | bytes 49160 | tf_op jit(solution)/shard_map/ppermute | solution.py:627
  3.8 1.3 divide_multiply_fusion.act_ref
  5.9 1.9 %convolution_add_fusion.1 = f32[4,768]{1,0:T(4,128)S(1)} fusion(f32[384,768]{1,0:T(8,128)} %refs_4_.1, f32[768]{0:T(1024)} %param.39, f32[1,4,384]{2,1,0:T(4,128)} %param.22), kind=kOutput, calls=%fused_computation.9 | convolution fusion | flops 14164992 | bytes 1201152 | tf_op jit(solution)/shard_map/dot_general | solution.py:758
  7.9 3.7 %convolution_add_fusion = f32[4,2304]{1,0:T(4,128)S(1)} fusion(f32[384,2304]{1,0:T(8,128)} %refs_3_.1, f32[2304]{0:T(1024)} %param.28, f32[1,4,384]{2,1,0:T(4,128)} %param.22), kind=kOutput, calls=%fused_computation | convolution fusion | flops 42482688 | bytes 3591168 | tf_op jit(solution)/shard_map/dot_general | solution.py:757
  11.6 0.6 fusion.2.refs_6_.mods_ref
  12.3 0.7 select_maximum_fusion.refs_8_
  13.0 0.1 collective-permute-start.2
  13.1 0.6 pad_add_fusion.refs_0_.meta
  13.8 0.8 copy.42.refs_15_
  14.6 0.6 copy-done.9
  15.2 16.4 %front.1 = (f32[32,256]{1,0:T(8,128)}, bf16[256,512]{1,0:T(8,128)(2,1)}, bf16[1024,1152]{1,0:T(8,128)(2,1)}, bf16[256,384]{1,0:T(8,128)(2,1)}, f32[256,384]{1,0:...) custom-call(s32[4]{0:T(128)} %pad_add_fusion.refs_0_.meta, ...), custom_call_target="tpu_custom_call" | custom-call | flops 16000000000 | tf_op jit(solution)/shard_map/front/pallas_call | solution.py:781
  31.6 4.4 %early_side.1 = bf16[2,1920,384]{2,1,0:T(8,128)(2,1)} custom-call(s32[4]{0:T(128)} %pad_add_fusion.refs_0_.meta, bf16[256,1536]{1,0:T(8,128)(2,1)} %get-tuple-element.71.activ, bf16[256,384]{1,0:T(8,128)(2,1)} %get-tuple-element.72.grad_mlp, bf16[256,384]{1,0:T(8,128)(2,1)} %get-tuple-element.73.entry_two, bf16[256,1536]{1,0:T(8,128)(2,1)} %get-tuple-element.74.grad_inner, ...), custom_call_target="tpu_custom_call" | custom-call | flops 3000000000 | tf_op jit(solution)/shard_map/early_side/pallas_call | solution.py:840
  36.0 1.6 %slice_bitcast_fusion = bf16[1920,384]{1,0:T(8,128)(2,1)S(1)} fusion(bf16[2,1920,384]{2,1,0:T(8,128)(2,1)} %early_side.1), kind=kLoop, calls=%fused_computation.3 | loop fusion | bytes 2949120 | tf_op jit(solution)/shard_map/squeeze | solution.py:660
  37.6 0.4 collective-permute-start.16
  38.0 0.1 collective-permute-start.4
  38.1 0.3 collective-permute-start.3
  38.4 5.7 %query_side.1.grad_query = bf16[256,384]{1,0:T(8,128)(2,1)} custom-call(s32[4]{0:T(128)} %pad_add_fusion.refs_0_.meta, bf16[1024,1152]{1,0:T(8,128)(2,1)} %get-tuple-element.61.qkv_all, bf16[256,512]{1,0:T(8,128)(2,1)} %get-tuple-element.62.payload.pay_own, f32[256,128]{1,0:T(8,128)} %get-tuple-element.63.stat_ref), custom_call_target="tpu_custom_call" | custom-call | flops 5000000000 | tf_op jit(solution)/shard_map/query_side/pallas_call | solution.py:861
  44.1 2.6 %collective-permute-done.3.pay_row = bf16[256,512]{1,0:T(8,128)(2,1)S(1)} collective-permute-done((bf16[256,512]{1,0:T(8,128)(2,1)S(1)}, bf16[256,512]{1,0:T(8,128)(2,1)S(1)}, u32[]{:S(2)}, u32[]{:S(2)}) %collective-permute-start.3) | collective-permute-done | bytes 262176 | tf_op jit(solution)/shard_map/ppermute | solution.py:627
  46.7 2.3 %fusion = bf16[1920,384]{1,0:T(8,128)(2,1)S(1)} fusion(bf16[1920,384]{1,0:T(8,128)(2,1)} %collective-permute-done.16, bf16[2,1920,384]{2,1,0:T(8,128)(2,1)} %early_side.1), kind=kLoop, calls=%fused_computation.2 | loop fusion | flops 2949120 | bytes 4423680 | tf_op jit(solution)/shard_map/convert_element_type | solution.py:661
  49.1 1.5 %collective-permute-start.17 = (bf16[960,384]{1,0:T(8,128)(2,1)S(1)}, bf16[960,384]{1,0:T(8,128)(2,1)}, u32[]{:S(2)}, u32[]{:S(2)}) collective-permute-start(bf16[960,384]{1,0:T(8,128)(2,1)S(1)} %constant_dynamic-slice_fusion.3), channel_id=1, source_target_pairs={{0,4},{1,9},{2,6},{3,11},{4,0},{5,13},{6,2},{7,15},{8,12},{9,1},{1... | collective-permute-start | bytes 2211848 | tf_op jit(solution)/shard_map/ppermute | solution.py:655
  50.7 0.7 copy-done.6
  51.5 9.3 %key_side.1 = (bf16[2,768,384]{2,1,0:T(8,128)(2,1)}, f32[16,256]{1,0:T(8,128)}) custom-call(s32[4]{0:T(128)} %pad_add_fusion.refs_0_.meta, bf16[1024,1152]{1,0:T(8,128)(2,1)} %get-tuple-element.61.qkv_all, bf16[256,512]{1,0:T(8,128)(2,1)} %get-tuple-element.62.payload.pay_own, bf16[256,512]{1,0:T(8,128)(2,1)} %copy-done.7, bf16[256,512]{1,0:T(8,128)(2,1)} %copy-done.6, ...), custom_call_target="tpu_custom_call" | custom-call | flops 8999999488 | tf_op jit(solution)/shard_map/key_side/pallas_call | solution.py:870
  60.8 1.4 add_convert_fusion
  62.2 0.8 constant_dynamic-slice_fusion.2
  63.0 0.5 collective-permute-start.18
  63.6 1.0 collective-permute-start.6
  64.6 6.3 %collective-permute-done.18 = bf16[480,384]{1,0:T(8,128)(2,1)} collective-permute-done((bf16[480,384]{1,0:T(8,128)(2,1)}, bf16[480,384]{1,0:T(8,128)(2,1)}, u32[]{:S(2)}, u32[]{:S(2)}) %collective-permute-start.18) | collective-permute-done | bytes 368672 | tf_op jit(solution)/shard_map/ppermute | solution.py:655
  70.8 1.1 add_convert_fusion.1
  71.9 1.6 %collective-permute-start.19 = (bf16[240,384]{1,0:T(8,128)(2,1)S(1)}, bf16[240,384]{1,0:T(8,128)(2,1)S(1)}, u32[]{:S(2)}, u32[]{:S(2)}) collective-permute-start(bf16[240,384]{1,0:T(8,128)(2,1)S(1)} %constant_dynamic-slice_fusion.1), channel_id=1, source_target_pairs={{0,8},{1,3},{2,10},{3,1},{4,12},{5,7},{6,14},{7,5},{8,0},{9,11},{1... | collective-permute-start | bytes 552968 | tf_op jit(solution)/shard_map/ppermute | solution.py:655
  73.6 0.1 fusion.1
  73.8 0.6 collective-permute-start.7
  74.4 3.2 %collective-permute-done.19 = bf16[240,384]{1,0:T(8,128)(2,1)S(1)} collective-permute-done((bf16[240,384]{1,0:T(8,128)(2,1)S(1)}, bf16[240,384]{1,0:T(8,128)(2,1)S(1)}, u32[]{:S(2)}, u32[]{:S(2)}) %collective-permute-start.19) | collective-permute-done | bytes 184352 | tf_op jit(solution)/shard_map/ppermute | solution.py:655
  77.6 2.7 %collective-permute-start.20 = (bf16[120,384]{1,0:T(8,128)(2,1)S(1)}, bf16[120,384]{1,0:T(8,128)(2,1)S(1)}, u32[]{:S(2)}, u32[]{:S(2)}) collective-permute-start(bf16[120,384]{1,0:T(8,128)(2,1)S(1)} %constant_dynamic-slice_fusion), channel_id=1, source_target_pairs={{0,16},{1,17},{2,18},{3,19},{4,20},{5,21},{6,22},{7,23},{8,24},{9,... | collective-permute-start | bytes 276488 | tf_op jit(solution)/shard_map/ppermute | solution.py:655
  80.3 0.3 collective-permute-done.7
  80.7 2.5 %collective-permute-done.20 = bf16[120,384]{1,0:T(8,128)(2,1)S(1)} collective-permute-done((bf16[120,384]{1,0:T(8,128)(2,1)S(1)}, bf16[120,384]{1,0:T(8,128)(2,1)S(1)}, u32[]{:S(2)}, u32[]{:S(2)}) %collective-permute-start.20) | collective-permute-done | bytes 92192 | tf_op jit(solution)/shard_map/ppermute | solution.py:655
  83.2 2.8 %collective-permute-start.21 = (bf16[120,384]{1,0:T(8,128)(2,1)S(1)}, bf16[120,384]{1,0:T(8,128)(2,1)S(1)}, u32[]{:S(2)}, u32[]{:S(2)}) collective-permute-start(bf16[120,384]{1,0:T(8,128)(2,1)S(1)} %add_convert_fusion.5), channel_id=1, source_target_pairs={{0,16},{1,17},{2,18},{3,19},{4,20},{5,21},{6,22},{7,23},{8,24},{9,... | collective-permute-start | bytes 276488 | tf_op jit(solution)/shard_map/ppermute | solution.py:655
  86.0 1.4 collective-permute-start.8
  87.4 1.3 collective-permute-done.21
  88.8 4.2 %collective-permute-start.22 = (bf16[240,384]{1,0:T(8,128)(2,1)S(1)}, bf16[240,384]{1,0:T(8,128)(2,1)S(1)}, u32[]{:S(2)}, u32[]{:S(2)}) collective-permute-start(bf16[240,384]{1,0:T(8,128)(2,1)S(1)} %pad_maximum_fusion.5), channel_id=1, source_target_pairs={{0,8},{1,3},{2,10},{3,1},{4,12},{5,7},{6,14},{7,5},{8,0},{9,11},{1... | collective-permute-start | bytes 552968 | tf_op jit(solution)/shard_map/ppermute | solution.py:655
  93.0 3.5 %collective-permute-done.22 = bf16[240,384]{1,0:T(8,128)(2,1)S(1)} collective-permute-done((bf16[240,384]{1,0:T(8,128)(2,1)S(1)}, bf16[240,384]{1,0:T(8,128)(2,1)S(1)}, u32[]{:S(2)}, u32[]{:S(2)}) %collective-permute-start.22) | collective-permute-done | bytes 184352 | tf_op jit(solution)/shard_map/ppermute | solution.py:655
  96.6 0.6 collective-permute-start.23
  97.2 2.1 %collective-permute-start.9 = (bf16[96,384]{1,0:T(8,128)(2,1)S(1)}, bf16[96,384]{1,0:T(8,128)(2,1)S(1)}, u32[]{:S(2)}, u32[]{:S(2)}) collective-permute-start(bf16[96,384]{1,0:T(8,128)(2,1)S(1)} %constant_dynamic-slice_fusion.5), channel_id=1, source_target_pairs={{0,8},{1,3},{2,10},{3,1},{4,12},{5,7},{6,14},{7,5},{8,0},{9,11},{1... | collective-permute-start | bytes 221192 | tf_op jit(solution)/shard_map/ppermute | solution.py:655
  99.2 3.1 %collective-permute-done.9 = bf16[96,384]{1,0:T(8,128)(2,1)S(1)} collective-permute-done((bf16[96,384]{1,0:T(8,128)(2,1)S(1)}, bf16[96,384]{1,0:T(8,128)(2,1)S(1)}, u32[]{:S(2)}, u32[]{:S(2)}) %collective-permute-start.9) | collective-permute-done | bytes 73760 | tf_op jit(solution)/shard_map/ppermute | solution.py:655
  102.4 1.8 %collective-permute-done.23 = bf16[480,384]{1,0:T(8,128)(2,1)S(1)} collective-permute-done((bf16[480,384]{1,0:T(8,128)(2,1)S(1)}, bf16[480,384]{1,0:T(8,128)(2,1)S(1)}, u32[]{:S(2)}, u32[]{:S(2)}) %collective-permute-start.23) | collective-permute-done | bytes 368672 | tf_op jit(solution)/shard_map/ppermute | solution.py:655
  104.2 0.1 broadcast_select_fusion.3
  104.4 1.4 collective-permute-start.24
  105.8 2.9 %collective-permute-start.10 = (bf16[48,384]{1,0:T(8,128)(2,1)S(1)}, bf16[48,384]{1,0:T(8,128)(2,1)S(1)}, u32[]{:S(2)}, u32[]{:S(2)}) collective-permute-start(bf16[48,384]{1,0:T(8,128)(2,1)S(1)} %constant_dynamic-slice_fusion.4), channel_id=1, source_target_pairs={{0,16},{1,17},{2,18},{3,19},{4,20},{5,21},{6,22},{7,23},{8,24},{9,... | collective-permute-start | bytes 110600 | tf_op jit(solution)/shard_map/ppermute | solution.py:655
  108.7 1.9 %collective-permute-done.10 = bf16[48,384]{1,0:T(8,128)(2,1)S(1)} collective-permute-done((bf16[48,384]{1,0:T(8,128)(2,1)S(1)}, bf16[48,384]{1,0:T(8,128)(2,1)S(1)}, u32[]{:S(2)}, u32[]{:S(2)}) %collective-permute-start.10) | collective-permute-done | bytes 36896 | tf_op jit(solution)/shard_map/ppermute | solution.py:655
  110.7 3.0 %collective-permute-start.11 = (bf16[48,384]{1,0:T(8,128)(2,1)S(1)}, bf16[48,384]{1,0:T(8,128)(2,1)S(1)}, u32[]{:S(2)}, u32[]{:S(2)}) collective-permute-start(bf16[48,384]{1,0:T(8,128)(2,1)S(1)} %add_convert_fusion.7), channel_id=1, source_target_pairs={{0,16},{1,17},{2,18},{3,19},{4,20},{5,21},{6,22},{7,23},{8,24},{9,... | collective-permute-start | bytes 110600 | tf_op jit(solution)/shard_map/ppermute | solution.py:655
  113.7 1.9 %collective-permute-done.11 = bf16[48,384]{1,0:T(8,128)(2,1)S(1)} collective-permute-done((bf16[48,384]{1,0:T(8,128)(2,1)S(1)}, bf16[48,384]{1,0:T(8,128)(2,1)S(1)}, u32[]{:S(2)}, u32[]{:S(2)}) %collective-permute-start.11) | collective-permute-done | bytes 36896 | tf_op jit(solution)/shard_map/ppermute | solution.py:655
  115.6 2.2 %collective-permute-start.12 = (bf16[96,384]{1,0:T(8,128)(2,1)S(1)}, bf16[96,384]{1,0:T(8,128)(2,1)S(1)}, u32[]{:S(2)}, u32[]{:S(2)}) collective-permute-start(bf16[96,384]{1,0:T(8,128)(2,1)S(1)} %pad_maximum_fusion.7), channel_id=1, source_target_pairs={{0,8},{1,3},{2,10},{3,1},{4,12},{5,7},{6,14},{7,5},{8,0},{9,11},{1... | collective-permute-start | bytes 221192 | tf_op jit(solution)/shard_map/ppermute | solution.py:655
  117.9 0.3 broadcast_select_fusion.1
  118.1 0.1 pad_maximum_fusion.refs_1_
  118.4 1.8 %collective-permute-done.12 = bf16[96,384]{1,0:T(8,128)(2,1)S(1)} collective-permute-done((bf16[96,384]{1,0:T(8,128)(2,1)S(1)}, bf16[96,384]{1,0:T(8,128)(2,1)S(1)}, u32[]{:S(2)}, u32[]{:S(2)}) %collective-permute-start.12) | collective-permute-done | bytes 73760 | tf_op jit(solution)/shard_map/ppermute | solution.py:655
  120.3 0.8 collective-permute-start.13
  121.0 4.4 %collective-permute-done.13 = bf16[192,384]{1,0:T(8,128)(2,1)S(1)} collective-permute-done((bf16[192,384]{1,0:T(8,128)(2,1)S(1)}, bf16[192,384]{1,0:T(8,128)(2,1)S(1)}, u32[]{:S(2)}, u32[]{:S(2)}) %collective-permute-start.13) | collective-permute-done | bytes 147488 | tf_op jit(solution)/shard_map/ppermute | solution.py:655
  125.6 0.6 collective-permute-start.14
  126.1 2.4 %slice.27.refs_6_ = f32[384,768]{1,0:T(8,128)} slice(f32[384,2304]{1,0:T(8,128)} %refs_3_.1), slice={[0:384], [0:768]} | slice | bytes 2359296 | tf_op jit(solution)/shard_map/slice | solution.py:965
  128.5 3.9 %collective-permute-done.14 = bf16[384,384]{1,0:T(8,128)(2,1)S(1)} collective-permute-done((bf16[384,384]{1,0:T(8,128)(2,1)S(1)}, bf16[384,384]{1,0:T(8,128)(2,1)S(1)}, u32[]{:S(2)}, u32[]{:S(2)}) %collective-permute-start.14) | collective-permute-done | bytes 294944 | tf_op jit(solution)/shard_map/ppermute | solution.py:655
  132.6 1.2 copy-done.4
  133.9 8.9 %unpack_early.1 = (f32[1536,384]{1,0:T(8,128)}, f32[384,384]{1,0:T(8,128)}, f32[384,1536]{1,0:T(8,128)}, f32[384,32]{1,0:T(8,128)}, f32[384]{0:T(512)}, /*index=...) custom-call(s32[4]{0:T(128)} %pad_add_fusion.refs_0_.meta, ...), custom_call_target="tpu_custom_call" | custom-call | flops 8000000000 | tf_op jit(solution)/shard_map/unpack_early/pallas_call | solution.py:908
  142.8 1.7 %copy.43 = f32[384,32]{0,1:T(8,128)} copy(f32[384,32]{1,0:T(8,128)} %get-tuple-element.118) | data formatting | bytes 98304
  144.4 4.3 %unpack_late.1 = (f32[384,2304]{1,0:T(8,128)}, f32[4,384]{1,0:T(4,128)}, f32[16,384]{1,0:T(8,128)}, f32[384]{0:T(512)}, f32[2304]{0:T(1024)}, /*index=5*/f32[384,1152]{1,0:T(8,128)}, f32[384]{0:T(512)}, f32[384]{0:T(512)}) custom-call(s32[4]{0:T(128)} %pad_add_fusion.refs_0_.meta, bf16[768,384]{1,0:T(8,128)(2,1)} %copy-done.2, ...), custom_call_target="tpu_custom_call", output_to_operand_aliasing={{0}: (7, {})} | custom-call | flops 5000000000 | tf_op jit(solution)/shard_map/unpack_late/pallas_call | solution.py:940
  (67 shorter events, 1.6 us)
Async XLA Ops:
  0.7 14.0 %collective-permute-start.1 = (f32[16,256]{1,0:T(8,128)}, f32[16,256]{1,0:T(8,128)S(1)}, u32[]{:S(2)}, u32[]{:S(2)}) collective-permute-start(f32[16,256]{1,0:T(8,128)} %bitcast.33), channel_id=1, source_target_pairs={{0,1},{1,0},{2,3},{3,2},{4,5},{5,4},{6,7},{7,6},{8,9},{9,8},{10,11... | collective-permute-start | bytes 49160 | tf_op jit(solution)/shard_map/ppermute | solution.py:627
  1.2 11.8 %collective-permute-start = (f32[16,256]{1,0:T(8,128)}, f32[16,256]{1,0:T(8,128)S(1)}, u32[]{:S(2)}, u32[]{:S(2)}) collective-permute-start(f32[16,256]{1,0:T(8,128)} %bitcast.34), channel_id=1, source_target_pairs={{0,2},{2,0},{1,3},{3,1},{4,6},{6,4},{5,7},{7,5},{8,10},{10,8},{9,1... | collective-permute-start | bytes 49160 | tf_op jit(solution)/shard_map/ppermute | solution.py:627
  7.9 5.9 %copy-start.3 = (f32[384,32]{0,1:T(8,128)S(1)}, f32[384,32]{0,1:T(8,128)}, u32[]{:S(2)}) copy-start(f32[384,32]{0,1:T(8,128)} %param.40) | copy-start | bytes 147460
  13.0 1.6 %copy-start.10 = (f32[16,256]{1,0:T(8,128)}, f32[16,256]{1,0:T(8,128)S(1)}, u32[]{:S(2)}) copy-start(f32[16,256]{1,0:T(8,128)S(1)} %collective-permute-done.refs_2_) | copy-start | bytes 49156
  13.0 1.6 %collective-permute-start.2 = (f32[16,256]{1,0:T(8,128)S(1)}, f32[16,256]{1,0:T(8,128)S(1)}, u32[]{:S(2)}, u32[]{:S(2)}) collective-permute-start(f32[16,256]{1,0:T(8,128)S(1)} %collective-permute-done.refs_2_), channel_id=1, source_target_pairs={{0,1},{1,0},{2,3},{3,2},{4,5},{5,4},{6,7},{7,6},{8,9},{9,8},{10,11... | collective-permute-start | bytes 49160 | tf_op jit(solution)/shard_map/ppermute | solution.py:627
  14.6 0.6 copy-start.9
  14.6 0.6 copy-start.11
  36.0 2.0 %copy-start.5 = (bf16[256,512]{1,0:T(8,128)(2,1)S(1)}, bf16[256,512]{1,0:T(8,128)(2,1)}, u32[]{:S(2)}) copy-start(bf16[256,512]{1,0:T(8,128)(2,1)} %get-tuple-element.62.payload.pay_own) | copy-start | bytes 786436
  37.6 9.2 %collective-permute-start.16 = (bf16[1920,384]{1,0:T(8,128)(2,1)S(1)}, bf16[1920,384]{1,0:T(8,128)(2,1)}, u32[]{:S(2)}, u32[]{:S(2)}) collective-permute-start(bf16[1920,384]{1,0:T(8,128)(2,1)S(1)} %slice_bitcast_fusion), channel_id=1, source_target_pairs={{0,1},{1,0},{2,3},{3,2},{4,5},{5,4},{6,7},{7,6},{8,9},{9,8},{10,11... | collective-permute-start | bytes 4423688 | tf_op jit(solution)/shard_map/ppermute | solution.py:627
  38.0 12.7 %collective-permute-start.4 = (bf16[256,512]{1,0:T(8,128)(2,1)S(1)}, bf16[256,512]{1,0:T(8,128)(2,1)S(1)}, u32[]{:S(2)}, u32[]{:S(2)}) collective-permute-start(bf16[256,512]{1,0:T(8,128)(2,1)S(1)} %copy-done.5), channel_id=1, source_target_pairs={{0,1},{1,0},{2,3},{3,2},{4,5},{5,4},{6,7},{7,6},{8,9},{9,8},{10,11... | collective-permute-start | bytes 786440 | tf_op jit(solution)/shard_map/ppermute | solution.py:627
  38.1 8.6 %collective-permute-start.3 = (bf16[256,512]{1,0:T(8,128)(2,1)S(1)}, bf16[256,512]{1,0:T(8,128)(2,1)S(1)}, u32[]{:S(2)}, u32[]{:S(2)}) collective-permute-start(bf16[256,512]{1,0:T(8,128)(2,1)S(1)} %copy-done.5), channel_id=1, source_target_pairs={{0,2},{2,0},{1,3},{3,1},{4,6},{6,4},{5,7},{7,5},{8,10},{10,8},{9,1... | collective-permute-start | bytes 786440 | tf_op jit(solution)/shard_map/ppermute | solution.py:627
  46.7 2.3 %copy-start.7 = (bf16[256,512]{1,0:T(8,128)(2,1)}, bf16[256,512]{1,0:T(8,128)(2,1)S(1)}, u32[]{:S(2)}) copy-start(bf16[256,512]{1,0:T(8,128)(2,1)S(1)} %collective-permute-done.3.pay_row) | copy-start | bytes 786436
  46.7 4.0 %collective-permute-start.5 = (bf16[256,512]{1,0:T(8,128)(2,1)S(1)}, bf16[256,512]{1,0:T(8,128)(2,1)S(1)}, u32[]{:S(2)}, u32[]{:S(2)}) collective-permute-start(bf16[256,512]{1,0:T(8,128)(2,1)S(1)} %collective-permute-done.3.pay_row), channel_id=1, source_target_pairs={{0,1},{1,0},{2,3},{3,2},{4,5},{5,4},{6,7},{7,6},{8,9},{9,8},{10,11... | collective-permute-start | bytes 786440 | tf_op jit(solution)/shard_map/ppermute | solution.py:627
  49.1 11.7 %collective-permute-start.17 = (bf16[960,384]{1,0:T(8,128)(2,1)S(1)}, bf16[960,384]{1,0:T(8,128)(2,1)}, u32[]{:S(2)}, u32[]{:S(2)}) collective-permute-start(bf16[960,384]{1,0:T(8,128)(2,1)S(1)} %constant_dynamic-slice_fusion.3), channel_id=1, source_target_pairs={{0,4},{1,9},{2,6},{3,11},{4,0},{5,13},{6,2},{7,15},{8,12},{9,1},{1... | collective-permute-start | bytes 2211848 | tf_op jit(solution)/shard_map/ppermute | solution.py:655
  50.7 0.7 copy-start.6
  50.7 0.8 copy-start.8
  60.8 2.7 %copy-start.1 = (bf16[2,768,384]{2,1,0:T(8,128)(2,1)S(1)}, bf16[2,768,384]{2,1,0:T(8,128)(2,1)}, u32[]{:S(2)}) copy-start(bf16[2,768,384]{2,1,0:T(8,128)(2,1)} %get-tuple-element.70) | copy-start | bytes 3538948
  63.0 7.8 %collective-permute-start.18 = (bf16[480,384]{1,0:T(8,128)(2,1)}, bf16[480,384]{1,0:T(8,128)(2,1)}, u32[]{:S(2)}, u32[]{:S(2)}) collective-permute-start(bf16[480,384]{1,0:T(8,128)(2,1)} %constant_dynamic-slice_fusion.2), channel_id=1, source_target_pairs={{0,2},{1,5},{2,0},{3,7},{4,6},{5,1},{6,4},{7,3},{8,10},{9,13},{10,... | collective-permute-start | bytes 1105928 | tf_op jit(solution)/shard_map/ppermute | solution.py:655
  63.6 10.0 %collective-permute-start.6 = (bf16[768,384]{1,0:T(8,128)(2,1)S(1)}, bf16[768,384]{1,0:T(8,128)(2,1)S(1)}, u32[]{:S(2)}, u32[]{:S(2)}) collective-permute-start(bf16[768,384]{1,0:T(8,128)(2,1)S(1)} %slice_bitcast_fusion.2), channel_id=1, source_target_pairs={{0,1},{1,0},{2,3},{3,2},{4,5},{5,4},{6,7},{7,6},{8,9},{9,8},{10,11... | collective-permute-start | bytes 1769480 | tf_op jit(solution)/shard_map/ppermute | solution.py:627
  71.9 5.6 %collective-permute-start.19 = (bf16[240,384]{1,0:T(8,128)(2,1)S(1)}, bf16[240,384]{1,0:T(8,128)(2,1)S(1)}, u32[]{:S(2)}, u32[]{:S(2)}) collective-permute-start(bf16[240,384]{1,0:T(8,128)(2,1)S(1)} %constant_dynamic-slice_fusion.1), channel_id=1, source_target_pairs={{0,8},{1,3},{2,10},{3,1},{4,12},{5,7},{6,14},{7,5},{8,0},{9,11},{1... | collective-permute-start | bytes 552968 | tf_op jit(solution)/shard_map/ppermute | solution.py:655
  73.8 6.8 %collective-permute-start.7 = (bf16[384,384]{1,0:T(8,128)(2,1)S(1)}, bf16[384,384]{1,0:T(8,128)(2,1)S(1)}, u32[]{:S(2)}, u32[]{:S(2)}) collective-permute-start(bf16[384,384]{1,0:T(8,128)(2,1)S(1)} %constant_dynamic-slice_fusion.7), channel_id=1, source_target_pairs={{0,2},{1,5},{2,0},{3,7},{4,6},{5,1},{6,4},{7,3},{8,10},{9,13},{10,... | collective-permute-start | bytes 884744 | tf_op jit(solution)/shard_map/ppermute | solution.py:655
  77.6 5.5 %collective-permute-start.20 = (bf16[120,384]{1,0:T(8,128)(2,1)S(1)}, bf16[120,384]{1,0:T(8,128)(2,1)S(1)}, u32[]{:S(2)}, u32[]{:S(2)}) collective-permute-start(bf16[120,384]{1,0:T(8,128)(2,1)S(1)} %constant_dynamic-slice_fusion), channel_id=1, source_target_pairs={{0,16},{1,17},{2,18},{3,19},{4,20},{5,21},{6,22},{7,23},{8,24},{9,... | collective-permute-start | bytes 276488 | tf_op jit(solution)/shard_map/ppermute | solution.py:655
  83.2 5.5 %collective-permute-start.21 = (bf16[120,384]{1,0:T(8,128)(2,1)S(1)}, bf16[120,384]{1,0:T(8,128)(2,1)S(1)}, u32[]{:S(2)}, u32[]{:S(2)}) collective-permute-start(bf16[120,384]{1,0:T(8,128)(2,1)S(1)} %add_convert_fusion.5), channel_id=1, source_target_pairs={{0,16},{1,17},{2,18},{3,19},{4,20},{5,21},{6,22},{7,23},{8,24},{9,... | collective-permute-start | bytes 276488 | tf_op jit(solution)/shard_map/ppermute | solution.py:655
  86.0 7.0 %collective-permute-start.8 = (bf16[192,384]{1,0:T(8,128)(2,1)S(1)}, bf16[192,384]{1,0:T(8,128)(2,1)S(1)}, u32[]{:S(2)}, u32[]{:S(2)}) collective-permute-start(bf16[192,384]{1,0:T(8,128)(2,1)S(1)} %constant_dynamic-slice_fusion.6), channel_id=1, source_target_pairs={{0,4},{1,9},{2,6},{3,11},{4,0},{5,13},{6,2},{7,15},{8,12},{9,1},{1... | collective-permute-start | bytes 442376 | tf_op jit(solution)/shard_map/ppermute | solution.py:655
  88.8 7.7 %collective-permute-start.22 = (bf16[240,384]{1,0:T(8,128)(2,1)S(1)}, bf16[240,384]{1,0:T(8,128)(2,1)S(1)}, u32[]{:S(2)}, u32[]{:S(2)}) collective-permute-start(bf16[240,384]{1,0:T(8,128)(2,1)S(1)} %pad_maximum_fusion.5), channel_id=1, source_target_pairs={{0,8},{1,3},{2,10},{3,1},{4,12},{5,7},{6,14},{7,5},{8,0},{9,11},{1... | collective-permute-start | bytes 552968 | tf_op jit(solution)/shard_map/ppermute | solution.py:655
  96.6 7.6 %collective-permute-start.23 = (bf16[480,384]{1,0:T(8,128)(2,1)S(1)}, bf16[480,384]{1,0:T(8,128)(2,1)S(1)}, u32[]{:S(2)}, u32[]{:S(2)}) collective-permute-start(bf16[480,384]{1,0:T(8,128)(2,1)S(1)} %pad_maximum_fusion.3), channel_id=1, source_target_pairs={{0,2},{1,5},{2,0},{3,7},{4,6},{5,1},{6,4},{7,3},{8,10},{9,13},{10,... | collective-permute-start | bytes 1105928 | tf_op jit(solution)/shard_map/ppermute | solution.py:655
  97.2 5.2 %collective-permute-start.9 = (bf16[96,384]{1,0:T(8,128)(2,1)S(1)}, bf16[96,384]{1,0:T(8,128)(2,1)S(1)}, u32[]{:S(2)}, u32[]{:S(2)}) collective-permute-start(bf16[96,384]{1,0:T(8,128)(2,1)S(1)} %constant_dynamic-slice_fusion.5), channel_id=1, source_target_pairs={{0,8},{1,3},{2,10},{3,1},{4,12},{5,7},{6,14},{7,5},{8,0},{9,11},{1... | collective-permute-start | bytes 221192 | tf_op jit(solution)/shard_map/ppermute | solution.py:655
  104.4 13.5 %collective-permute-start.24 = (bf16[960,384]{1,0:T(8,128)(2,1)S(1)}, bf16[960,384]{1,0:T(8,128)(2,1)S(1)}, u32[]{:S(2)}, u32[]{:S(2)}) collective-permute-start(bf16[960,384]{1,0:T(8,128)(2,1)S(1)} %pad_maximum_fusion.1), channel_id=1, source_target_pairs={{0,4},{1,9},{2,6},{3,11},{4,0},{5,13},{6,2},{7,15},{8,12},{9,1},{1... | collective-permute-start | bytes 2211848 | tf_op jit(solution)/shard_map/ppermute | solution.py:655
  105.8 4.9 %collective-permute-start.10 = (bf16[48,384]{1,0:T(8,128)(2,1)S(1)}, bf16[48,384]{1,0:T(8,128)(2,1)S(1)}, u32[]{:S(2)}, u32[]{:S(2)}) collective-permute-start(bf16[48,384]{1,0:T(8,128)(2,1)S(1)} %constant_dynamic-slice_fusion.4), channel_id=1, source_target_pairs={{0,16},{1,17},{2,18},{3,19},{4,20},{5,21},{6,22},{7,23},{8,24},{9,... | collective-permute-start | bytes 110600 | tf_op jit(solution)/shard_map/ppermute | solution.py:655
  110.7 4.9 %collective-permute-start.11 = (bf16[48,384]{1,0:T(8,128)(2,1)S(1)}, bf16[48,384]{1,0:T(8,128)(2,1)S(1)}, u32[]{:S(2)}, u32[]{:S(2)}) collective-permute-start(bf16[48,384]{1,0:T(8,128)(2,1)S(1)} %add_convert_fusion.7), channel_id=1, source_target_pairs={{0,16},{1,17},{2,18},{3,19},{4,20},{5,21},{6,22},{7,23},{8,24},{9,... | collective-permute-start | bytes 110600 | tf_op jit(solution)/shard_map/ppermute | solution.py:655
  115.6 4.5 %collective-permute-start.12 = (bf16[96,384]{1,0:T(8,128)(2,1)S(1)}, bf16[96,384]{1,0:T(8,128)(2,1)S(1)}, u32[]{:S(2)}, u32[]{:S(2)}) collective-permute-start(bf16[96,384]{1,0:T(8,128)(2,1)S(1)} %pad_maximum_fusion.7), channel_id=1, source_target_pairs={{0,8},{1,3},{2,10},{3,1},{4,12},{5,7},{6,14},{7,5},{8,0},{9,11},{1... | collective-permute-start | bytes 221192 | tf_op jit(solution)/shard_map/ppermute | solution.py:655
  118.3 10.2 %copy-start = (bf16[1920,384]{1,0:T(8,128)(2,1)}, bf16[1920,384]{1,0:T(8,128)(2,1)S(1)}, u32[]{:S(2)}) copy-start(bf16[1920,384]{1,0:T(8,128)(2,1)S(1)} %pad_maximum_fusion.refs_1_) | copy-start | bytes 4423684
  118.3 14.3 %collective-permute-start.25 = (bf16[1920,384]{1,0:T(8,128)(2,1)S(1)}, bf16[1920,384]{1,0:T(8,128)(2,1)S(1)}, u32[]{:S(2)}, u32[]{:S(2)}) collective-permute-start(bf16[1920,384]{1,0:T(8,128)(2,1)S(1)} %pad_maximum_fusion.refs_1_), channel_id=1, source_target_pairs={{0,1},{1,0},{2,3},{3,2},{4,5},{5,4},{6,7},{7,6},{8,9},{9,8},{10,11... | collective-permute-start | bytes 4423688 | tf_op jit(solution)/shard_map/ppermute | solution.py:627
  120.3 5.2 %collective-permute-start.13 = (bf16[192,384]{1,0:T(8,128)(2,1)S(1)}, bf16[192,384]{1,0:T(8,128)(2,1)S(1)}, u32[]{:S(2)}, u32[]{:S(2)}) collective-permute-start(bf16[192,384]{1,0:T(8,128)(2,1)S(1)} %pad_maximum_fusion.6), channel_id=1, source_target_pairs={{0,4},{1,9},{2,6},{3,11},{4,0},{5,13},{6,2},{7,15},{8,12},{9,1},{1... | collective-permute-start | bytes 442376 | tf_op jit(solution)/shard_map/ppermute | solution.py:655
  125.6 6.8 %collective-permute-start.14 = (bf16[384,384]{1,0:T(8,128)(2,1)S(1)}, bf16[384,384]{1,0:T(8,128)(2,1)S(1)}, u32[]{:S(2)}, u32[]{:S(2)}) collective-permute-start(bf16[384,384]{1,0:T(8,128)(2,1)S(1)} %pad_maximum_fusion.4), channel_id=1, source_target_pairs={{0,2},{1,5},{2,0},{3,7},{4,6},{5,1},{6,4},{7,3},{8,10},{9,13},{10,... | collective-permute-start | bytes 884744 | tf_op jit(solution)/shard_map/ppermute | solution.py:655
  132.5 10.2 %copy-start.2 = (bf16[768,384]{1,0:T(8,128)(2,1)}, bf16[768,384]{1,0:T(8,128)(2,1)S(1)}, u32[]{:S(2)}) copy-start(bf16[768,384]{1,0:T(8,128)(2,1)S(1)} %pad_maximum_fusion.2.refs_1_) | copy-start | bytes 1769476
  132.5 11.9 %collective-permute-start.15 = (bf16[768,384]{1,0:T(8,128)(2,1)S(1)}, bf16[768,384]{1,0:T(8,128)(2,1)}, u32[]{:S(2)}, u32[]{:S(2)}) collective-permute-start(bf16[768,384]{1,0:T(8,128)(2,1)S(1)} %pad_maximum_fusion.2.refs_1_), channel_id=1, source_target_pairs={{0,1},{1,0},{2,3},{3,2},{4,5},{5,4},{6,7},{7,6},{8,9},{9,8},{10,11... | collective-permute-start | bytes 1769480 | tf_op jit(solution)/shard_map/ppermute | solution.py:627
  132.6 1.2 copy-start.4
